TPU v7x, 32 devices: a whole 2x2x4 slice. The times are simulated.
32 devices in a mesh: groups: 1, seq: 32 (over z, y, x, core).
Axes of the slice: x: 2, y: 2, z: 4, core: 2. Of those that a mesh axis runs over, the one named last changes fastest.
Arguments:
- tokens: bfloat16 [8192, 1024], P(('groups', 'seq')), may hold values from -6 to 6
- values: bfloat16 [8192, 2048], P(('groups', 'seq')), may hold values from -6 to 6
- in_weight: bfloat16 [1024, 288], replicated, may hold values from -0.059814453 to 0.059814453
- step_bias: float32 [32], replicated, may hold values from -4.5 to -3
- decay_log: float32 [32], replicated, may hold values from -9 to 1
- skip_gain: float32 [32], replicated, may hold values from 0.5 to 1.5
- trace_lengths: int32 [4], P('groups'), may hold values from 1 to 4096, 8192 in all
- output_grad: bfloat16 [8192, 2048], P(('groups', 'seq')), may hold values from -6 to 6
Outputs:
- output: bfloat16 [8192, 2048], P(('groups', 'seq'))
- grad_values: bfloat16 [8192, 2048], P(('groups', 'seq'))
- grad_tokens: bfloat16 [8192, 1024], P(('groups', 'seq'))
- grad_in_weight: float32 [1024, 288], P('groups')
- grad_heads: float32 [3, 32], P('groups')
Inputs may be any that keep to these rules, and one draw needn't show every extreme that they name: `trace_lengths`: the lengths of the 4 traces packed in order; they sum to 8192 and the longest has exactly 4096 tokens.
All inputs are finite; a program needn't handle non-finite values.
Results may differ from a plain program's by a relative error of at most 0.012.
Values sent between devices are 32-bit elements; how exact they have to be, the bound alone decides.
A program may use at most 320 MiB of HBM per device.

v0:
```python
from functools import partial

import jax
import jax.numpy as jnp
from jax import lax
from jax.sharding import PartitionSpec as P


def entering(x, axis, combine, identity, reverse):
    length, here = (lax.axis_size(axis), lax.axis_index(axis))
    everything = jax.tree.map(lambda part: lax.all_gather(part, axis), x)
    start = jax.tree.map(
        lambda part, zero: jnp.broadcast_to(jnp.asarray(zero, part.dtype), part.shape), x, identity
    )

    def lap(k, before):
        at = length - 1 - k if reverse else k
        reached = at > here if reverse else at < here
        new = combine(before, jax.tree.map(lambda part: part[at], everything))
        return jax.tree.map(lambda a, b: jnp.where(reached, a, b), new, before)

    return lax.fori_loop(0, length, lap, start)


def trace_ids(trace_lengths, first_row, count):
    trace_ends = jnp.cumsum(trace_lengths)
    position = first_row + jnp.arange(count, dtype=jnp.int32)
    return jnp.sum((position[:, None] >= trace_ends[None, :]).astype(jnp.int32), axis=1)


def prepare(projected, values, step_bias, decay_log, trace_index, carrying):
    head_count = step_bias.shape[0]
    row_count = values.shape[0]
    head_width = values.shape[1] // head_count
    state_size = (projected.shape[1] - head_count) // 2
    input_map = projected[:, :state_size].astype(jnp.bfloat16)
    output_map = projected[:, state_size : 2 * state_size].astype(jnp.bfloat16)
    step_sizes = jax.nn.softplus(projected[:, 2 * state_size :] + step_bias[None, :])
    decays = jnp.cumsum(-jnp.exp(decay_log)[None, :] * step_sizes, axis=0)
    total_decay = decays[-1]
    tail_mask = (trace_index == trace_index[-1]).astype(jnp.float32)
    tail_weight = jnp.exp(total_decay[None, :] - decays) * step_sizes * tail_mask[:, None]
    weighted = (values.reshape(row_count, head_count, head_width) * tail_weight[:, :, None]).astype(
        jnp.bfloat16
    )
    summary = jnp.einsum("lhp,ln->hpn", weighted, input_map, preferred_element_type=jnp.float32)
    retained = jnp.exp(total_decay) * carrying[-1]
    return (input_map, output_map, step_sizes, decays, retained, summary)


def head_block(pieces, linked, scores):
    block_decay, block_steps, block_vals = pieces
    group_size = block_decay.shape[0]
    row_count = block_vals.shape[0]
    log_gaps = jnp.where(linked[None] > 0.5, block_decay[:, :, None] - block_decay[:, None, :], 0.0)
    mixing = (jnp.exp(log_gaps) * linked[None] * scores[None] * block_steps[:, None, :]).astype(
        jnp.bfloat16
    )
    head_vals = block_vals.reshape(row_count, group_size, -1)
    mixed = jnp.einsum("hij,jhp->ihp", mixing, head_vals, preferred_element_type=jnp.float32)
    return mixed.reshape(row_count, -1)


def respond(
    input_map,
    output_map,
    step_sizes,
    decays,
    values,
    skip_gain,
    incoming,
    trace_index,
    carrying,
    kernel,
):
    head_count = step_sizes.shape[1]
    row_count = values.shape[0]
    head_width = values.shape[1] // head_count
    group_size = min(8, head_count)
    block_count = head_count // group_size
    scores = jnp.dot(output_map, input_map.T, preferred_element_type=jnp.float32)
    position = jnp.arange(row_count, dtype=jnp.int32)
    linked = (
        (position[:, None] >= position[None, :]) & (trace_index[:, None] == trace_index[None, :])
    ).astype(jnp.float32)
    group_decay = decays.T.reshape(block_count, group_size, row_count)
    group_steps = step_sizes.T.reshape(block_count, group_size, row_count)
    group_vals = values.reshape(row_count, block_count, group_size * head_width).transpose(1, 0, 2)
    mixed = lax.map(
        lambda pieces: kernel(pieces, linked, scores), (group_decay, group_steps, group_vals)
    )
    intra = mixed.transpose(1, 0, 2).reshape(row_count, head_count, head_width)
    carried = jnp.einsum(
        "ln,hpn->lhp", output_map.astype(jnp.float32), incoming, precision=lax.Precision.HIGH
    )
    decay_rows = jnp.exp(decays) * carrying[:, None]
    direct = skip_gain[None, :, None] * values.reshape(row_count, head_count, head_width).astype(
        jnp.float32
    )
    result = intra + carried * decay_rows[:, :, None] + direct
    return result.reshape(row_count, head_count * head_width)


def compose(earlier, later):
    return (earlier[0] * later[0], later[1] + later[0][:, None, None] * earlier[1])


def shards(tokens, values, in_weight, step_bias, decay_log, skip_gain, trace_lengths, output_grad):
    row_count = tokens.shape[0]
    head_count = step_bias.shape[0]
    head_width = values.shape[1] // head_count
    state_size = (in_weight.shape[1] - head_count) // 2
    first_row = lax.axis_index("seq") * row_count
    trace_index = trace_ids(trace_lengths, first_row, row_count)
    prior_trace = trace_ids(trace_lengths, first_row - 1, 1)[0]
    carrying = (trace_index == prior_trace).astype(jnp.float32)
    projected = jnp.dot(tokens, in_weight, preferred_element_type=jnp.float32)
    first_section = partial(prepare, trace_index=trace_index, carrying=carrying)
    (input_map, output_map, step_sizes, decays, retained, summary), pull_first = jax.vjp(
        first_section, projected, values, step_bias, decay_log
    )
    unit_gate = jnp.ones((head_count,), jnp.float32)
    zero_state = jnp.zeros((head_count, head_width, state_size), jnp.float32)
    incoming = entering((retained, summary), "seq", compose, (unit_gate, zero_state), False)[1]
    kernel = jax.checkpoint(head_block)
    second_section = partial(respond, trace_index=trace_index, carrying=carrying, kernel=kernel)
    output_raw, pull_second = jax.vjp(
        second_section, input_map, output_map, step_sizes, decays, values, skip_gain, incoming
    )
    grads_second = pull_second(output_grad.astype(jnp.float32))
    adjoint_seed = grads_second[6]
    adjoint = entering((retained, adjoint_seed), "seq", compose, (unit_gate, zero_state), True)[1]
    grad_retained = jnp.sum(adjoint * incoming, axis=(1, 2))
    grads_first = pull_first(
        (grads_second[0], grads_second[1], grads_second[2], grads_second[3], grad_retained, adjoint)
    )
    grad_projected, grad_vals_first, grad_bias, grad_decay = grads_first
    grad_values = grad_vals_first + grads_second[4]
    grad_skip = grads_second[5]
    grad_rounded = grad_projected.astype(jnp.bfloat16)
    grad_tokens = jnp.dot(grad_rounded, in_weight.T, preferred_element_type=jnp.float32).astype(
        jnp.bfloat16
    )
    weight_part = lax.dot_general(
        tokens, grad_rounded, (((0,), (0,)), ((), ())), preferred_element_type=jnp.float32
    )
    head_part = jnp.stack([grad_bias, grad_decay, grad_skip])
    grad_in_weight, grad_heads = lax.psum((weight_part, head_part), "seq")
    return (output_raw.astype(jnp.bfloat16), grad_values, grad_tokens, grad_in_weight, grad_heads)


def solution(mesh):
    in_specs = (
        P(("groups", "seq"), None),
        P(("groups", "seq"), None),
        P(),
        P(),
        P(),
        P(),
        P("groups"),
        P(("groups", "seq"), None),
    )
    out_specs = (
        P(("groups", "seq"), None),
        P(("groups", "seq"), None),
        P(("groups", "seq"), None),
        P("groups", None),
        P("groups", None),
    )
    return jax.shard_map(shards, mesh=mesh, in_specs=in_specs, out_specs=out_specs, check_vma=False)
```

profile of v0, /device:TPU:0, one launch (start us, length us, event | category | flops | bytes accessed | tf_op | source)
XLA Modules:
  0.0 653.5 jit_solution(61655767618022578)
XLA Ops:
  16.1 1.5 copy.148
  17.6 1.7 fusion.43
  19.5 1.5 copy.142
  21.0 1.6 fusion.60
  22.7 2.3 copy.137
  25.7 2.8 convert.25
  30.4 43.8 %all-gather.2 = f32[32,1,32]{2,1,0:T(1,128)S(1)} all-gather(f32[1,1,32]{2,1,0:T(1,128)S(1)} %get-tuple-element.770), channel_id=1, replica_groups=mesh['groups'=1,'seq'=32] {'seq'}, dimensions={0}, use_global_device_ids=true | all-gather | bytes 4224 | tf_op jit(solution)/shard_map/all_gather | solution.py:11
  75.8 141.2 %all-gather.8.cloned.1.call-done = f32[1024,64,128]{2,1,0:T(8,128)} async-done(((f32[32,64,128]{2,1,0:T(8,128)}), f32[1024,64,128]{2,1,0:T(8,128)}) %all-gather.8.cloned.1.call-update) | async-done | bytes 33554448 | tf_op jit(solution)/shard_map/all_gather | solution.py:11
  217.0 49.3 %while.65 = (s32[]{:T(128)}, f32[32,64,128]{2,1,0:T(8,128)S(1)}, s32[]{:T(128)}, f32[32,32,64,128]{3,2,1,0:T(8,128)}, f32[32,32]{1,0:T(8,128)S(1)}, /*index=5*/s32[]{:T(128)}, s32[]{:T(128)}, s32[]{:T(128)}, s32[]{:T(128)}) while((s32[]{:T(128)}, f32[32,64,128]{2,1,0:T(8,128)S(1)}, s32[]{:T(128)}, ...), condition=%wide.region_10.11_spmd.clone, body=%wide.region_9.10_spmd.clone.sunk | while | flops 1048584 | bytes 3146279 | solution.py:22
  220.1 1.5 fusion.119
  223.1 1.5 fusion.119
  224.6 1.6 fusion.119
  226.2 1.6 fusion.119
  227.9 1.7 fusion.119
  232.6 1.5 fusion.119
  234.2 1.5 fusion.119
  235.7 1.5 fusion.119
  240.3 1.5 fusion.119
  241.8 1.5 fusion.119
  243.3 1.5 fusion.119
  247.9 1.5 fusion.119
  250.9 1.5 fusion.119
  258.5 1.8 fusion.119
  264.8 1.5 fusion.119
  266.9 3.0 fusion.40
  273.6 30.7 %while.66 = (s32[]{:T(128)}, f32[256,256]{1,0:T(8,128)S(1)}, f32[4,8,256]{2,1,0:T(8,128)}, f32[4,8,256]{2,1,0:T(8,128)}, bf16[4,256,512]{1,2,0:T(8,128)(2,1)}, /...) while((s32[]{:T(128)}, f32[256,256]{1,0:T(8,128)S(1)}, ...), condition=%wide.region_16.17_spmd.clone, body=%wide.region_11.16_spmd.clone.sunk | while | flops 146143232 | bytes 6620363 | solution.py:89
  275.6 1.8 convolution_convert_fusion.7
  278.1 1.9 fusion.124
  283.3 1.8 convolution_convert_fusion.7
  285.8 1.9 fusion.124
  290.9 1.8 convolution_convert_fusion.7
  293.5 1.9 fusion.124
  298.6 1.8 convolution_convert_fusion.7
  301.2 1.9 fusion.124
  304.3 1.6 convolution_convert_fusion.5
  306.0 1.7 convolution_convert_fusion.4
  307.7 105.2 %all-gather.6.cloned.1.call-done = f32[1024,64,128]{2,1,0:T(8,128)} async-done(((f32[32,64,128]{2,1,0:T(8,128)}), f32[1024,64,128]{2,1,0:T(8,128)}) %all-gather.6.cloned.1.call-update) | async-done | bytes 33554448 | tf_op jit(solution)/shard_map/all_gather | solution.py:11
  412.9 69.1 %while.64 = (s32[]{:T(128)}, f32[32,64,128]{2,1,0:T(8,128)S(1)}, s32[]{:T(128)}, f32[32,32,64,128]{3,2,1,0:T(8,128)}, f32[32,32]{1,0:T(8,128)}, /*index=5*/s32[]{:T(128)}, s32[]{:T(128)}) while((s32[]{:T(128)}, f32[32,64,128]{2,1,0:T(8,128)S(1)}, s32[]{:T(128)}, f32[32,32,64,128]{3,2,1,0:T(8,128)}, f32[32,32]{1,0:T(8,128)}, ...), condition=%wide.region_8.9_spmd.clone, body=%wide.region_7.8_spmd.clone.sunk | while | flops 1048580 | bytes 3146217 | solution.py:22
  483.0 13.7 %while.63 = (s32[]{:T(128)}, f32[4,256,512]{1,2,0:T(8,128)}, bf16[4,256,512]{1,2,0:T(8,128)(2,1)}, f32[4,8,256]{2,1,0:T(8,128)}, f32[1,256,256]{2,1,0:T(8,128)S(...) while((s32[]{:T(128)}, f32[4,256,512]{1,2,0:T(8,128)}, ...), condition=%wide.region_5.6_spmd.clone, body=%wide.region_4.5_spmd.clone.sunk | while | flops 70516736 | bytes 3262053 | solution.py:89
  496.8 4.9 multiply_reduce_fusion.1
  502.6 2.5 reduce-window.21
  506.3 3.6 fusion.52
  513.0 2.1 convolution_convert_fusion.3
  516.6 2.4 copy.153
  520.3 38.6 %psum.15 = f32[3,32]{1,0:T(4,128)} all-reduce(f32[3,32]{1,0:T(4,128)S(1)} %pad_maximum_fusion), channel_id=1, replica_groups=mesh['groups'=1,'seq'=32] {'seq'}, use_global_device_ids=true, to_apply=%region_28.29 | all-reduce | flops 96 | bytes 768 | tf_op jit(solution)/shard_map/psum | solution.py:148
  559.0 3.1 fusion.57
  562.0 82.5 %all-reduce.6.cloned.1.call-done = f32[1024,288]{0,1:T(8,128)} async-done(((f32[1024,288]{0,1:T(8,128)}), f32[1024,288]{0,1:T(8,128)}) %all-reduce.6.cloned.1.call-update) | async-done | bytes 1179664 | tf_op jit(solution)/shard_map/psum | solution.py:148
  644.5 2.4 copy.226
  (304 shorter events, 149.5 us)
Async XLA Ops:
  7.2 4.1 copy-start
  7.2 8.7 %copy-start.20 = (f32[32]{0:T(128)S(1)}, f32[32]{0:T(128)}, u32[]{:S(2)}) copy-start(f32[32]{0:T(128)} %param.19) | copy-start | bytes 388
  7.2 209.8 %all-gather.8.cloned.1.call-start = ((), (), s32[]{:S(2)}) async-start(), calls=%async_computation.2 | async-start | bytes 34603008 | tf_op jit(solution)/shard_map/all_gather | solution.py:11
  10.7 5.3 copy-start.24
  12.7 254.2 %copy-start.9 = (bf16[256,288]{0,1:T(8,128)(2,1)}, bf16[256,288]{0,1:T(8,128)(2,1)S(1)}, u32[]{:S(2)}) copy-start(bf16[256,288]{0,1:T(8,128)(2,1)S(1)} %get-tuple-element.774) | copy-start | bytes 442372
  13.5 1.4 copy-start.30
  15.9 254.2 %copy-start.22 = (f32[32]{0:T(128)}, f32[32]{0:T(128)S(1)}, u32[]{:S(2)}) copy-start(f32[32]{0:T(128)S(1)} %get-tuple-element.771) | copy-start | bytes 388
  17.6 1.7 copy-start.1
  19.3 393.5 %all-gather.6.cloned.1.call-start = ((), (), s32[]{:S(2)}) async-start(), calls=%async_computation.1 | async-start | bytes 34603008 | tf_op jit(solution)/shard_map/all_gather | solution.py:11
  21.0 1.7 copy-start.2
  22.6 621.9 %all-reduce.6.cloned.1.call-start = ((), (), s32[]{:S(2)}) async-start(), calls=%async_computation | async-start | bytes 2359296 | tf_op jit(solution)/shard_map/psum | solution.py:148
  25.6 2.8 copy-start.4
  25.6 2.8 copy-start.5
  25.6 3.3 copy-start.26
  266.3 0.6 copy-start.19
  270.1 3.6 copy-start.11
  275.6 2.6 copy-start.14
  283.2 2.6 copy-start.14
  290.9 2.6 copy-start.14
  298.6 2.6 copy-start.14
  482.0 0.9 copy-start.16
  482.0 1.0 copy-start.15
  482.0 1.0 copy-start.17
  496.7 5.0 copy-start.27
  496.7 5.0 copy-start.28
  496.7 5.6 copy-start.12
  496.8 5.6 copy-start.21
  496.8 5.6 copy-start.23
  496.8 5.6 copy-start.25
  506.3 3.6 copy-start.3
  509.9 1.7 copy-start.13
  509.9 1.4 copy-start.31
  509.9 1.7 copy-start.10
  511.4 3.7 copy-start.32
  511.6 3.5 copy-start.29
  511.6 3.5 copy-start.8
  515.1 3.8 copy-start.7
  516.5 42.4 %copy-start.6 = (bf16[256,2048]{1,0:T(8,128)(2,1)S(1)}, bf16[256,2048]{1,0:T(8,128)(2,1)}, u32[]{:S(2)}) copy-start(bf16[256,2048]{1,0:T(8,128)(2,1)} %param.23) | copy-start | bytes 3145732
  516.5 42.4 %copy-start.18 = (f32[2048]{0:T(1024)S(1)}, f32[2048]{0:T(1024)}, u32[]{:S(2)}) copy-start(f32[2048]{0:T(1024)} %mul.406) | copy-start | bytes 24580
Sparse Core Ops, SparseCore 0:
  19.5 197.5 all-gather.7
  219.9 192.9 all-gather.5
  515.2 129.2 all-reduce.5
where the time goes:
time: 658 us; the launch traced here: 653 us
  waiting for transfers between devices  329 us (50%)
  other arithmetic  116 us (18%)
  blocking collectives  82.4 us (13%)
  local copies, waits for them, and re-layouts  65.9 us (10%)
  matrix products  43.2 us (7%)
  between operations  14.2 us (2%)
    all_gather x2, waiting for transfers between devices, entering(): everything = jax.tree.map(lambda part: lax.all_gather(part, axis), x)  246 us
    select_n x64, other arithmetic, lap(): return jax.tree.map(lambda a, b: jnp.where(reached, a, b), new, before)  94.3 us
    psum x1, waiting for transfers between devices, shards(): grad_in_weight, grad_heads = lax.psum((weight_part, head_part), 'seq')  82.5 us
    all_gather x1, blocking collectives, entering(): everything = jax.tree.map(lambda part: lax.all_gather(part, axis), x)  43.8 us
    psum x1, blocking collectives, shards(): grad_in_weight, grad_heads = lax.psum((weight_part, head_part), 'seq')  38.6 us
    mul x64, local copies, waits for them, and re-layouts, compose(): later[0][:, None, None] * earlier[1]  22.2 us
    dot_general x12, matrix products, head_block(): jnp.einsum('hij,jhp->ihp', mixing, head_vals, preferred_element_type=jnp....  18 us
  transfers between devices with their start and end apart: 3, of which 3 were waited for; matrix products, arithmetic and copies ran while one was open for 17% of the time, Pallas kernels for 0%

commit v1 on v0

--- a/solution.py
+++ b/solution.py
@@ -3,23 +3,324 @@
 import jax
 import jax.numpy as jnp
 from jax import lax
+from jax.experimental import pallas as pl
+from jax.experimental.pallas import tpu as pltpu
 from jax.sharding import PartitionSpec as P
 
 
-def entering(x, axis, combine, identity, reverse):
-    length, here = (lax.axis_size(axis), lax.axis_index(axis))
-    everything = jax.tree.map(lambda part: lax.all_gather(part, axis), x)
-    start = jax.tree.map(
-        lambda part, zero: jnp.broadcast_to(jnp.asarray(zero, part.dtype), part.shape), x, identity
-    )
-
-    def lap(k, before):
-        at = length - 1 - k if reverse else k
-        reached = at > here if reverse else at < here
-        new = combine(before, jax.tree.map(lambda part: part[at], everything))
-        return jax.tree.map(lambda a, b: jnp.where(reached, a, b), new, before)
-
-    return lax.fori_loop(0, length, lap, start)
+MESH = pl.DeviceIdType.MESH
+CORES = 2
+CHIPS = 4
+
+
+def placing(length):
+    here = lax.axis_index("seq")
+    core = lax.rem(here, CORES)
+    chip = lax.rem(lax.div(here, CORES), CHIPS)
+    plane = lax.div(here, CORES * CHIPS)
+    return core, chip, plane, length // (CORES * CHIPS)
+
+
+def device_at(plane, chip, core):
+    return {"seq": (plane * CHIPS + chip) * CORES + core}
+
+
+def greet(core, chip, plane, planes):
+    barrier = pltpu.get_barrier_semaphore()
+    others = [device_at(plane, chip, 1 - core)]
+    others += [device_at(plane, lax.rem(chip + d, CHIPS), core) for d in range(1, CHIPS)]
+    others += [device_at(lax.rem(plane + d, planes), chip, core) for d in range(1, planes)]
+    for other in others:
+        pl.semaphore_signal(barrier, inc=1, device_id=other, device_id_type=MESH)
+    pl.semaphore_wait(barrier, len(others))
+
+
+def sending(src, dst, send, recv, at, to):
+    return pltpu.make_async_remote_copy(
+        src_ref=src,
+        dst_ref=dst,
+        send_sem=send.at[at],
+        recv_sem=recv.at[at],
+        device_id=to,
+        device_id_type=MESH,
+    )
+
+
+def scan_kernel(length, width, own, out, pair, half, quad, part, zf, zb, gate, back, held, away,
+                send, recv, keep):
+    core, chip, plane, planes = placing(length)
+    greet(core, chip, plane, planes)
+    w = width
+    heads = own.shape[0]
+    mid, low = heads // CORES, heads // (CORES * CHIPS)
+    partner = device_at(plane, chip, 1 - core)
+
+    cp = sending(own.at[pl.ds((1 - core) * mid, mid)], pair.at[core], send, recv, 0, partner)
+    cp.start()
+    mine = pltpu.make_async_copy(own.at[pl.ds(core * mid, mid)], pair.at[core], keep.at[0])
+    mine.start()
+    mine.wait()
+    cp.wait()
+    first, second = 0, 1
+
+    def join(h, _):
+        f0, r0 = pair[first, h, 0:w], pair[first, h, w : w + 8]
+        f1, r1 = pair[second, h, 0:w], pair[second, h, w : w + 8]
+        a0, a1 = pair[first, h, w + 8 :], pair[second, h, w + 8 :]
+        half[h, 0:w] = f1 + r1[0:1] * f0
+        half[h, w : w + 8] = r0 * r1
+        half[h, w + 8 :] = a0 + r0[0:1] * a1
+        return 0
+
+    lax.fori_loop(0, mid, join, 0)
+
+    copies = []
+    for d in range(1, CHIPS):
+        to = lax.rem(chip + d, CHIPS)
+        cp = sending(
+            half.at[pl.ds(to * low, low)], quad.at[chip], send, recv, d, device_at(plane, to, core)
+        )
+        cp.start()
+        copies.append(cp)
+    mine = pltpu.make_async_copy(half.at[pl.ds(chip * low, low)], quad.at[chip], keep.at[1])
+    mine.start()
+    mine.wait()
+    for cp in copies:
+        cp.wait()
+
+    def total(h, _):
+        f, r = quad[0, h, 0:w], quad[0, h, w : w + 8]
+        a = quad[CHIPS - 1, h, w + 8 :]
+        for c in range(1, CHIPS):
+            rc = quad[c, h, w : w + 8]
+            f = quad[c, h, 0:w] + rc[0:1] * f
+            r = r * rc
+            e = CHIPS - 1 - c
+            a = quad[e, h, w + 8 :] + quad[e, h, w : w + 1] * a
+        part[h, 0:w] = f
+        part[h, w : w + 8] = r
+        part[h, w + 8 :] = a
+        gate[h] = jnp.zeros((2 * w, gate.shape[2]), jnp.float32)
+        return 0
+
+    lax.fori_loop(0, low, total, 0)
+
+    base = CHIPS
+    ups, downs = [], []
+    for d in range(1, planes):
+        up = sending(
+            part.at[:, 0 : w + 8], zf.at[d - 1], send, recv, base + d,
+            device_at(lax.rem(plane + d, planes), chip, core),
+        )
+        down = sending(
+            part.at[:, w : 2 * w + 8], zb.at[d - 1], send, recv, base + planes + d,
+            device_at(lax.rem(plane + planes - d, planes), chip, core),
+        )
+        pl.when(plane + d < planes)(up.start)
+        pl.when(plane - d >= 0)(down.start)
+        ups.append(up)
+        downs.append(down)
+    for d in range(planes - 1, 0, -1):
+
+        @pl.when(plane - d >= 0)
+        def _():
+            ups[d - 1].wait_recv()
+
+            def add(h, _):
+                gate[h, 0:w] = zf[d - 1, h, 0:w] + zf[d - 1, h, w : w + 1] * gate[h, 0:w]
+                return 0
+
+            lax.fori_loop(0, low, add, 0)
+
+        @pl.when(plane + d < planes)
+        def _():
+            downs[d - 1].wait_recv()
+
+            def add(h, _):
+                gate[h, w:] = zb[d - 1, h, 8:] + zb[d - 1, h, 0:1] * gate[h, w:]
+                return 0
+
+            lax.fori_loop(0, low, add, 0)
+
+    def spread(h, _):
+        f, a = gate[h, 0:w], gate[h, w:]
+        for c in range(CHIPS):
+            e = CHIPS - 1 - c
+            back[c, h, 0:w] = f
+            back[e, h, w:] = a
+            if c < CHIPS - 1:
+                f = quad[c, h, 0:w] + quad[c, h, w : w + 1] * f
+                a = quad[e, h, w + 8 :] + quad[e, h, w : w + 1] * a
+        return 0
+
+    lax.fori_loop(0, low, spread, 0)
+    base = CHIPS + 2 * planes
+    copies = []
+    for d in range(1, CHIPS):
+        to = lax.rem(chip + d, CHIPS)
+        cp = sending(
+            back.at[to], held.at[pl.ds(chip * low, low)], send, recv, base + d,
+            device_at(plane, to, core),
+        )
+        cp.start()
+        copies.append(cp)
+    mine = pltpu.make_async_copy(back.at[chip], held.at[pl.ds(chip * low, low)], keep.at[2])
+    mine.start()
+    mine.wait()
+    for cp in copies:
+        cp.wait()
+
+    def last(h, _):
+        f, a = held[h, 0:w], held[h, w:]
+        f1 = pair[first, h, 0:w] + pair[first, h, w : w + 1] * f
+        a0 = pair[second, h, w + 8 :] + pair[second, h, w : w + 1] * a
+        early = core == 0
+        away[h, 0:w] = jnp.where(early, f1, f)
+        away[h, w:] = jnp.where(early, a, a0)
+        out[core * mid + h, 0:w] = jnp.where(early, f, f1)
+        out[core * mid + h, w:] = jnp.where(early, a0, a)
+        return 0
+
+    lax.fori_loop(0, mid, last, 0)
+    cp = sending(away, out.at[pl.ds(core * mid, mid)], send, recv, base + CHIPS, partner)
+    cp.start()
+    for d in range(1, planes):
+        pl.when(plane + d < planes)(ups[d - 1].wait_send)
+        pl.when(plane - d >= 0)(downs[d - 1].wait_send)
+    cp.wait()
+
+
+def scan_states(summary, seed, retained, length):
+    heads, width, state = summary.shape
+    gates = jnp.broadcast_to(retained[:, None, None], (heads, 8, state))
+    own = jnp.concatenate([summary, gates, seed], axis=1)
+    tall = 2 * width + 8
+    planes = length // (CORES * CHIPS)
+    mid, low = heads // CORES, heads // (CORES * CHIPS)
+    count = 2 * CHIPS + 2 * planes + 1
+    vmem = lambda *shape: pltpu.VMEM(shape, jnp.float32)
+    out = pl.pallas_call(
+        partial(scan_kernel, length, width),
+        out_shape=jax.ShapeDtypeStruct((heads, 2 * width, state), jnp.float32),
+        in_specs=[pl.BlockSpec(memory_space=pltpu.VMEM)],
+        out_specs=pl.BlockSpec(memory_space=pltpu.VMEM),
+        scratch_shapes=[
+            vmem(CORES, mid, tall, state),
+            vmem(mid, tall, state),
+            vmem(CHIPS, low, tall, state),
+            vmem(low, tall, state),
+            vmem(planes - 1, low, width + 8, state),
+            vmem(planes - 1, low, width + 8, state),
+            vmem(low, 2 * width, state),
+            vmem(CHIPS, low, 2 * width, state),
+            vmem(mid, 2 * width, state),
+            vmem(mid, 2 * width, state),
+            pltpu.SemaphoreType.DMA((count,)),
+            pltpu.SemaphoreType.DMA((count,)),
+            pltpu.SemaphoreType.DMA((3,)),
+        ],
+        compiler_params=pltpu.CompilerParams(
+            collective_id=0, has_side_effects=True, vmem_limit_bytes=48 << 20
+        ),
+    )(own)
+    return out[:, :width], out[:, width:]
+
+
+def sum_kernel(length, own, out, pair, half, quad, part, deep, send, recv):
+    core, chip, plane, planes = placing(length)
+    greet(core, chip, plane, planes)
+    rows = own.shape[0]
+    n1, n2, n3 = rows // CORES, rows // (CORES * CHIPS), rows // length
+    partner = device_at(plane, chip, 1 - core)
+
+    def across(copies):
+        for cp in copies:
+            cp.start()
+        for cp in copies:
+            cp.wait()
+
+    across([sending(own.at[pl.ds((1 - core) * n1, n1)], pair, send, recv, 0, partner)])
+
+    def first(i, _):
+        at = pl.multiple_of(i * 64, 64)
+        half[pl.ds(at, 64)] = own[pl.ds(core * n1 + at, 64)] + pair[pl.ds(at, 64)]
+        return 0
+
+    lax.fori_loop(0, n1 // 64, first, 0)
+    chips = [lax.rem(chip + d, CHIPS) for d in range(1, CHIPS)]
+    across(
+        [
+            sending(half.at[pl.ds(to * n2, n2)], quad.at[d], send, recv, 1 + d, device_at(plane, to, core))
+            for d, to in enumerate(chips)
+        ]
+    )
+
+    def second(i, _):
+        at = pl.multiple_of(i * 64, 64)
+        total = half[pl.ds(chip * n2 + at, 64)]
+        for d in range(CHIPS - 1):
+            total = total + quad[d, pl.ds(at, 64)]
+        part[pl.ds(at, 64)] = total
+        return 0
+
+    lax.fori_loop(0, n2 // 64, second, 0)
+    others = [lax.rem(plane + d, planes) for d in range(1, planes)]
+    across(
+        [
+            sending(part.at[pl.ds(to * n3, n3)], deep.at[d], send, recv, CHIPS + d, device_at(to, chip, core))
+            for d, to in enumerate(others)
+        ]
+    )
+    total = part[pl.ds(plane * n3, n3)]
+    for d in range(planes - 1):
+        total = total + deep[d]
+    at = core * n1 + chip * n2
+    out[pl.ds(at + plane * n3, n3)] = total
+    base = CHIPS + planes
+    block = out.at[pl.ds(at + plane * n3, n3)]
+    across(
+        [
+            sending(block, block, send, recv, base + d, device_at(to, chip, core))
+            for d, to in enumerate(others)
+        ]
+    )
+    block = out.at[pl.ds(at, n2)]
+    base += planes
+    across(
+        [
+            sending(block, block, send, recv, base + d, device_at(plane, to, core))
+            for d, to in enumerate(chips)
+        ]
+    )
+    block = out.at[pl.ds(core * n1, n1)]
+    base += CHIPS
+    across([sending(block, block, send, recv, base, partner)])
+
+
+def sum_all(stack, length):
+    rows, lanes = stack.shape
+    planes = length // (CORES * CHIPS)
+    n1, n2, n3 = rows // CORES, rows // (CORES * CHIPS), rows // length
+    count = 2 * CHIPS + 2 * planes + 1
+    vmem = lambda *shape: pltpu.VMEM(shape, jnp.float32)
+    return pl.pallas_call(
+        partial(sum_kernel, length),
+        out_shape=jax.ShapeDtypeStruct((rows, lanes), jnp.float32),
+        in_specs=[pl.BlockSpec(memory_space=pltpu.VMEM)],
+        out_specs=pl.BlockSpec(memory_space=pltpu.VMEM),
+        scratch_shapes=[
+            vmem(n1, lanes),
+            vmem(n1, lanes),
+            vmem(CHIPS - 1, n2, lanes),
+            vmem(n2, lanes),
+            vmem(planes - 1, n3, lanes),
+            pltpu.SemaphoreType.DMA((count,)),
+            pltpu.SemaphoreType.DMA((count,)),
+        ],
+        compiler_params=pltpu.CompilerParams(
+            collective_id=1, has_side_effects=True, vmem_limit_bytes=48 << 20
+        ),
+    )(stack)
 
 
 def trace_ids(trace_lengths, first_row, count):
@@ -119,17 +420,19 @@
     (input_map, output_map, step_sizes, decays, retained, summary), pull_first = jax.vjp(
         first_section, projected, values, step_bias, decay_log
     )
-    unit_gate = jnp.ones((head_count,), jnp.float32)
-    zero_state = jnp.zeros((head_count, head_width, state_size), jnp.float32)
-    incoming = entering((retained, summary), "seq", compose, (unit_gate, zero_state), False)[1]
+    length = lax.axis_size("seq")
+    decay_rows = jnp.exp(decays) * carrying[:, None]
+    scaled = (
+        output_grad.reshape(row_count, head_count, head_width) * decay_rows[:, :, None]
+    ).astype(jnp.bfloat16)
+    seed = jnp.einsum("lhp,ln->hpn", scaled, output_map, preferred_element_type=jnp.float32)
+    incoming, adjoint = scan_states(summary, seed, retained, length)
     kernel = jax.checkpoint(head_block)
     second_section = partial(respond, trace_index=trace_index, carrying=carrying, kernel=kernel)
     output_raw, pull_second = jax.vjp(
         second_section, input_map, output_map, step_sizes, decays, values, skip_gain, incoming
     )
     grads_second = pull_second(output_grad.astype(jnp.float32))
-    adjoint_seed = grads_second[6]
-    adjoint = entering((retained, adjoint_seed), "seq", compose, (unit_gate, zero_state), True)[1]
     grad_retained = jnp.sum(adjoint * incoming, axis=(1, 2))
     grads_first = pull_first(
         (grads_second[0], grads_second[1], grads_second[2], grads_second[3], grad_retained, adjoint)
@@ -142,10 +445,17 @@
         jnp.bfloat16
     )
     weight_part = lax.dot_general(
-        tokens, grad_rounded, (((0,), (0,)), ((), ())), preferred_element_type=jnp.float32
-    )
-    head_part = jnp.stack([grad_bias, grad_decay, grad_skip])
-    grad_in_weight, grad_heads = lax.psum((weight_part, head_part), "seq")
+        grad_rounded, tokens, (((0,), (0,)), ((), ())), preferred_element_type=jnp.float32
+    )
+    columns, width = weight_part.shape
+    head_part = jnp.concatenate([grad_bias, grad_decay, grad_skip])
+    head_rows = -(-(columns + 1) // 64) * 64 - columns
+    head_part = jnp.pad(head_part[None, :], ((0, head_rows - 1), (0, width - 3 * head_count)))
+    stack = jnp.concatenate([weight_part, head_part])
+    stack = stack.reshape(-1, width // 128, 128).transpose(1, 0, 2).reshape(-1, 128)
+    stack = sum_all(stack, length).reshape(width // 128, -1, 128)
+    grad_in_weight = stack[:, :columns].transpose(0, 2, 1).reshape(width, columns)
+    grad_heads = stack[0, columns, : 3 * head_count].reshape(3, head_count)
     return (output_raw.astype(jnp.bfloat16), grad_values, grad_tokens, grad_in_weight, grad_heads)
 
 

time: 658 us -> 218 us (0.33)
  waiting for transfers between devices: 329 us -> 0 us
  Pallas kernels: 0 us -> 84.1 us
  other arithmetic: 116 us -> 31.9 us
  blocking collectives: 82.4 us -> 0 us
  between operations: 14.2 us -> 1.17 us
  local copies, waits for them, and re-layouts: 65.9 us -> 54.6 us
    all_gather x2 -> x0, waiting for transfers between devices: 246 us -> none  [entering(): everything = jax.tree.map(lambda part: lax.all_gather(part, axis), x)]
    select_n x64 -> x0, other arithmetic: 94.3 us -> none  [lap(): return jax.tree.map(lambda a, b: jnp.where(reached, a, b), new, before)]
    pallas_call x0 -> x2, Pallas kernels: none -> 84.1 us  [the longest x1 52.3 us: scan_states(): pl.pallas_call(partial(scan_kernel, length, width), out_shape=jax.ShapeDt...]
    psum x1 -> x0, waiting for transfers between devices: 82.5 us -> none  [shards(): grad_in_weight, grad_heads = lax.psum((weight_part, head_part), 'seq')]
    all_gather x1 -> x0, blocking collectives: 43.8 us -> none  [entering(): everything = jax.tree.map(lambda part: lax.all_gather(part, axis), x)]
    psum x1 -> x0, blocking collectives: 38.6 us -> none  [shards(): grad_in_weight, grad_heads = lax.psum((weight_part, head_part), 'seq')]
    mul x65 -> x1, local copies, waits for them, and re-layouts: 22.3 us -> 0.08 us  [shards(): decay_rows = jnp.exp(decays) * carrying[:, None]]
    dot_general x12, matrix products: 18 us -> 27.8 us  [head_block(): jnp.einsum('hij,jhp->ihp', mixing, head_vals, preferred_element_type=jnp....]
  transfers between devices with their start and end apart: 3 -> 0, of which waited for: 3 -> 0; matrix products, arithmetic and copies ran while one was open for 17% -> 0% of each run, Pallas kernels for 0% -> 0%
where the time goes in v1:
time: 218 us; the launch traced here: 216 us
  Pallas kernels  84.1 us (39%)
  local copies, waits for them, and re-layouts  54.6 us (25%)
  matrix products  43.8 us (20%)
  other arithmetic  31.9 us (15%)
    pallas_call x1, Pallas kernels, scan_states(): pl.pallas_call(partial(scan_kernel, length, width), out_shape=jax.ShapeDt...  52.3 us
    pallas_call x1, Pallas kernels, sum_all(): pl.pallas_call(partial(sum_kernel, length), out_shape=jax.ShapeDtypeStruc...  31.7 us
    dot_general x12, matrix products, head_block(): jnp.einsum('hij,jhp->ihp', mixing, head_vals, preferred_element_type=jnp....  27.8 us
    dynamic_update_slice x12, local copies, waits for them, and re-layouts, respond(): lax.map(lambda pieces: kernel(pieces, linked, scores), (group_decay, grou...  11.4 us
    dot_general x2, matrix products, respond(): jnp.einsum('ln,hpn->lhp', output_map.astype(jnp.float32), incoming, preci...  7.2 us
    squeeze x8, local copies, waits for them, and re-layouts, respond(): lax.map(lambda pieces: kernel(pieces, linked, scores), (group_decay, grou...  7.15 us
    another operation x10, local copies, waits for them, and re-layouts  6.43 us
    another operation x7, other arithmetic  6.05 us

profile of v1, /device:TPU:0, one launch (start us, length us, event | category | flops | bytes accessed | tf_op | source)
XLA Modules:
  0.0 215.8 jit_solution(7177490345961540217)
XLA Ops:
  0.6 1.5 copy.138
  2.2 3.1 %copy.134 = f32[256,2048]{0,1:T(8,128)} copy(bf16[256,2048]{1,0:T(8,128)(2,1)} %param.13) | data formatting | bytes 3145728 | tf_op jit(solution)/shard_map/jvp()/convert_element_type | solution.py:344
  5.4 2.3 %copy.129 = bf16[256,2048]{0,1:T(8,128)(2,1)} copy(bf16[256,2048]{1,0:T(8,128)(2,1)} %param.13) | data formatting | bytes 2097152 | tf_op args[1]
  7.7 1.4 fusion.95
  13.5 1.3 compare_convert_fusion.2
  17.5 52.3 %shard_map.119 = f32[32,128,128]{2,1,0:T(8,128)S(1)} custom-call(f32[32,136,128]{2,1,0:T(8,128)S(1)} %pad_maximum_fusion.own), custom_call_target="tpu_custom_call" | custom-call | tf_op jit(solution)/shard_map/pallas_call | solution.py:202
  69.8 1.4 fusion.38
  72.9 17.6 %while.33 = (s32[]{:T(128)}, f32[4,256,512]{1,2,0:T(8,128)}, bf16[4,256,512]{1,2,0:T(8,128)(2,1)}, f32[4,8,256]{2,1,0:T(8,128)}, f32[1,256,256]{2,1,0:T(8,128)},...) while((s32[]{:T(128)}, f32[4,256,512]{1,2,0:T(8,128)}, ...), condition=%wide.region_5.6_spmd.clone, body=%wide.region_4.5_spmd.clone.sunk | while | flops 70516736 | bytes 3261553 | solution.py:390
  74.7 1.7 fusion.115
  79.1 1.7 fusion.115
  83.5 1.7 fusion.115
  87.9 1.7 fusion.115
  90.5 5.4 %multiply_reduce_fusion.1 = (f32[256,32]{0,1:T(8,128)}, bf16[256,32,64]{0,2,1:T(8,128)(2,1)}) fusion(f32[256,2048]{0,1:T(8,128)} %copy-done.1, f32[256,32,64]{0,2,1:T(8,128)} %bitcast.203, f32[32]{0:T(128)S(1)} %copy-done.29, f32[256,32,64]{0,2,1:T(8,128)} %bitcast.219, f32[256,32]{0,1:T(8,128)S(1)} %copy.139, f32[32,128,128]{2,1,0:T(8,128)S(1)} %shard_map.119, ...), kind=kOutput, calls=%fused_computation.63 | convolution fusion | flops 406315008 | bytes 8520192 | tf_op jit(solution)/shard_map/jvp(ln,hpn->lhp)/dot_general | solution.py:394
  95.9 2.3 %copy.158 = bf16[256,2048]{1,0:T(8,128)(2,1)} copy(bf16[256,2048]{0,1:T(8,128)(2,1)} %bitcast.213) | data formatting | bytes 2097152
  98.1 2.3 %copy.145 = bf16[256,2048]{1,0:T(8,128)(2,1)} copy(bf16[256,2048]{0,1:T(8,128)(2,1)} %bitcast.215) | data formatting | bytes 2097152 | tf_op jit(solution)/shard_map/transpose(jvp())/reshape | solution.py:344
  100.4 2.7 %convert.20 = bf16[4,256,512]{1,2,0:T(8,128)(2,1)} convert(f32[4,256,512]{1,2,0:T(8,128)} %bitcast.201) | non-fusion elementwise | flops 524288 | bytes 3145728
  105.4 46.0 %while.34 = (s32[]{:T(128)}, f32[256,256]{1,0:T(8,128)S(1)}, f32[4,8,256]{2,1,0:T(8,128)}, f32[4,8,256]{2,1,0:T(8,128)}, bf16[4,256,512]{1,2,0:T(8,128)(2,1)}, /...) while((s32[]{:T(128)}, f32[256,256]{1,0:T(8,128)S(1)}, ...), condition=%wide.region_12.13_spmd.clone, body=%wide.region_7.12_spmd.clone.sunk | while | flops 146143232 | bytes 5637359 | solution.py:390
  107.3 3.5 %fusion.120 = (f32[8,256]{1,0:T(8,128)S(1)}, f32[8,256]{1,0:T(8,128)}, f32[8,256]{1,0:T(8,128)}, f32[256,256]{1,0:T(8,128)}) fusion(f32[256,256]{1,0:T(8,128)} %get-tuple-element.623, f32[8,256]{1,0:T(8,128)S(1)} %get-tuple-element.624, f32[256,256]{1,0:T(8,128)S(1)} %fusion.119, f32[8,256]{1,0:T(8,128)S(1)} %get-tuple-element.626, ...), kind=kOutput, calls=%fused_computation.34.clone.1 | convolution fusion | flops 75425792 | bytes 1417216 | tf_op jit(solution)/shard_map/transpose(jvp())/while/body/eval_jaxpr/checkpoint/hij,jhp->ihp/dot_general | solution.py:361
  111.8 1.3 bitcast_dynamic-update-slice_fusion.4
  113.1 1.3 bitcast_dynamic-update-slice_fusion.5
  114.4 1.7 convolution_convert_fusion.7
  118.8 3.5 %fusion.120 = (f32[8,256]{1,0:T(8,128)S(1)}, f32[8,256]{1,0:T(8,128)}, f32[8,256]{1,0:T(8,128)}, f32[256,256]{1,0:T(8,128)}) fusion(f32[256,256]{1,0:T(8,128)} %get-tuple-element.623, f32[8,256]{1,0:T(8,128)S(1)} %get-tuple-element.624, f32[256,256]{1,0:T(8,128)S(1)} %fusion.119, f32[8,256]{1,0:T(8,128)S(1)} %get-tuple-element.626, ...), kind=kOutput, calls=%fused_computation.34.clone.1 | convolution fusion | flops 75425792 | bytes 1417216 | tf_op jit(solution)/shard_map/transpose(jvp())/while/body/eval_jaxpr/checkpoint/hij,jhp->ihp/dot_general | solution.py:361
  123.3 1.3 bitcast_dynamic-update-slice_fusion.4
  124.6 1.3 bitcast_dynamic-update-slice_fusion.5
  125.9 1.7 convolution_convert_fusion.7
  130.3 3.5 %fusion.120 = (f32[8,256]{1,0:T(8,128)S(1)}, f32[8,256]{1,0:T(8,128)}, f32[8,256]{1,0:T(8,128)}, f32[256,256]{1,0:T(8,128)}) fusion(f32[256,256]{1,0:T(8,128)} %get-tuple-element.623, f32[8,256]{1,0:T(8,128)S(1)} %get-tuple-element.624, f32[256,256]{1,0:T(8,128)S(1)} %fusion.119, f32[8,256]{1,0:T(8,128)S(1)} %get-tuple-element.626, ...), kind=kOutput, calls=%fused_computation.34.clone.1 | convolution fusion | flops 75425792 | bytes 1417216 | tf_op jit(solution)/shard_map/transpose(jvp())/while/body/eval_jaxpr/checkpoint/hij,jhp->ihp/dot_general | solution.py:361
  134.8 1.3 bitcast_dynamic-update-slice_fusion.4
  136.1 1.3 bitcast_dynamic-update-slice_fusion.5
  137.4 1.7 convolution_convert_fusion.7
  141.8 3.5 %fusion.120 = (f32[8,256]{1,0:T(8,128)S(1)}, f32[8,256]{1,0:T(8,128)}, f32[8,256]{1,0:T(8,128)}, f32[256,256]{1,0:T(8,128)}) fusion(f32[256,256]{1,0:T(8,128)} %get-tuple-element.623, f32[8,256]{1,0:T(8,128)S(1)} %get-tuple-element.624, f32[256,256]{1,0:T(8,128)S(1)} %fusion.119, f32[8,256]{1,0:T(8,128)S(1)} %get-tuple-element.626, ...), kind=kOutput, calls=%fused_computation.34.clone.1 | convolution fusion | flops 75425792 | bytes 1417216 | tf_op jit(solution)/shard_map/transpose(jvp())/while/body/eval_jaxpr/checkpoint/hij,jhp->ihp/dot_general | solution.py:361
  146.3 1.3 bitcast_dynamic-update-slice_fusion.4
  147.6 1.3 bitcast_dynamic-update-slice_fusion.5
  148.9 1.7 convolution_convert_fusion.7
  151.4 2.3 %copy.172 = bf16[256,2048]{1,0:T(8,128)(2,1)} copy(bf16[256,2048]{0,1:T(8,128)(2,1)} %bitcast.214) | data formatting | bytes 2097152 | tf_op jit(solution)/shard_map/transpose(jvp())/reshape | solution.py:389
  153.8 3.4 %fusion.55 = bf16[256,2048]{1,0:T(8,128)(2,1)} fusion(bf16[256,2048]{1,0:T(8,128)(2,1)} %copy.145, bf16[256,2048]{1,0:T(8,128)(2,1)} %copy.172, bf16[256,2048]{1,0:T(8,128)(2,1)} %param.19, f32[2048]{0:T(1024)S(1)} %mul.360), kind=kLoop, calls=%fused_computation.88 | loop fusion | flops 2621440 | bytes 4202496 | tf_op jit(solution)/shard_map/add | solution.py:441
  158.3 1.7 bitcast_add_fusion.2
  160.8 1.8 fusion.71
  162.6 1.6 copy.150
  164.2 3.2 %reduce-window.21 = f32[32,2,128]{2,0,1:T(8,128)S(1)} reduce-window(f32[32,2,128]{2,0,1:T(8,128)} %copy.150, f32[]{:T(128)} %constant.109.clone.1), window={size=1x1x128 pad=0_0x0_0x0_127}, to_apply=%region_17.18 | reduce-window | flops 1040384 | bytes 65540 | tf_op jit(solution)/shard_map/reduce-window.3
  168.1 1.3 reduce-window.24
  170.7 1.5 copy.151
  172.3 1.5 copy.146
  173.8 1.2 fusion.93
  175.2 2.3 %fusion.52 = bf16[256,128]{1,0:T(8,128)(2,1)S(1)} fusion(bf16[256,128]{1,0:T(8,128)(2,1)S(1)} %convolution_convert_fusion.4, f32[32,128,128]{2,1,0:T(8,128)S(1)} %shard_map.119, f32[256,32,64]{0,2,1:T(8,128)} %bitcast.204, f32[256,32]{0,1:T(8,128)S(1)} %copy-done.18), kind=kOutput, calls=%fused_computation.85 | convolution fusion | flops 135299072 | bytes 2785280 | tf_op jit(solution)/shard_map/transpose(jvp(lhp,ln->hpn))/dot_general | solution.py:347
  177.7 1.8 fusion.49
  179.6 1.2 convolution_convert_fusion.3
  182.2 31.7 %shard_map.120 = f32[2560,128]{1,0:T(8,128)S(1)} custom-call(f32[2560,128]{1,0:T(8,128)S(1)} %bitcast.197), custom_call_target="tpu_custom_call" | custom-call | tf_op jit(solution)/shard_map/pallas_call | solution.py:306
  213.9 1.2 copy_bitcast_fusion.1
  (177 shorter events, 42.5 us)
Async XLA Ops:
  0.6 7.0 %copy-start = (bf16[1024,288]{0,1:T(8,128)(2,1)S(1)}, bf16[1024,288]{0,1:T(8,128)(2,1)}, u32[]{:S(2)}) copy-start(bf16[1024,288]{0,1:T(8,128)(2,1)} %param.14) | copy-start | bytes 1769476
  2.2 12.9 %copy-start.1 = (f32[256,2048]{0,1:T(8,128)}, f32[256,2048]{0,1:T(8,128)S(1)}, u32[]{:S(2)}) copy-start(f32[256,2048]{0,1:T(8,128)S(1)} %copy.138) | copy-start | bytes 6291460
  2.2 5.5 %copy-start.32 = (f32[32]{0:T(128)S(1)}, f32[32]{0:T(128)}, u32[]{:S(2)}) copy-start(f32[32]{0:T(128)} %param.16) | copy-start | bytes 388
  5.4 3.9 %copy-start.26 = (f32[32]{0:T(128)S(1)}, f32[32]{0:T(128)}, u32[]{:S(2)}) copy-start(f32[32]{0:T(128)} %param.15) | copy-start | bytes 388
  5.4 6.6 %copy-start.31 = (s32[4]{0:T(128)S(1)}, s32[4]{0:T(128)}, u32[]{:S(2)}) copy-start(s32[4]{0:T(128)} %param.18) | copy-start | bytes 52
  7.7 1.7 copy-start.30
  9.1 81.4 %copy-start.10 = (bf16[256,288]{0,1:T(8,128)(2,1)}, bf16[256,288]{0,1:T(8,128)(2,1)S(1)}, u32[]{:S(2)}) copy-start(bf16[256,288]{0,1:T(8,128)(2,1)S(1)} %get-tuple-element.483) | copy-start | bytes 442372
  9.2 62.1 %copy-start.6 = (f32[256,32]{1,0:T(8,128)}, f32[256,32]{1,0:T(8,128)S(1)}, u32[]{:S(2)}) copy-start(f32[256,32]{1,0:T(8,128)S(1)} %copy.175) | copy-start | bytes 98308
  12.0 59.4 %copy-start.8 = (f32[32,2,128]{0,2,1:T(8,128)}, f32[32,2,128]{0,2,1:T(8,128)S(1)}, u32[]{:S(2)}) copy-start(f32[32,2,128]{0,2,1:T(8,128)S(1)} %copy.135) | copy-start | bytes 98308
  12.0 59.4 %copy-start.28 = (f32[32]{0:T(128)}, f32[32]{0:T(128)S(1)}, u32[]{:S(2)}) copy-start(f32[32]{0:T(128)S(1)} %slice_bitcast_fusion.1) | copy-start | bytes 388
  14.8 2.0 copy-start.27
  14.8 56.6 %copy-start.25 = (f32[256]{0:T(256)}, f32[256]{0:T(256)S(1)}, u32[]{:S(2)}) copy-start(f32[256]{0:T(256)S(1)} %get-tuple-element.481) | copy-start | bytes 3076
  15.0 54.8 %copy-start.17 = (f32[256,32]{0,1:T(8,128)}, f32[256,32]{0,1:T(8,128)S(1)}, u32[]{:S(2)}) copy-start(f32[256,32]{0,1:T(8,128)S(1)} %copy.136) | copy-start | bytes 98308
  15.1 75.4 %copy-start.15 = (f32[256,32]{0,1:T(8,128)}, f32[256,32]{0,1:T(8,128)S(1)}, u32[]{:S(2)}) copy-start(f32[256,32]{0,1:T(8,128)S(1)} %copy.139) | copy-start | bytes 98308
  15.1 1.7 copy-start.3
  71.4 1.5 copy-start.13
  72.9 17.6 %copy-start.29 = (f32[32]{0:T(128)S(1)}, f32[32]{0:T(128)}, u32[]{:S(2)}) copy-start(f32[32]{0:T(128)} %param.17) | copy-start | bytes 388
  106.1 4.7 %copy-start.21 = (f32[8,256]{1,0:T(8,128)}, f32[8,256]{1,0:T(8,128)S(1)}, u32[]{:S(2)}) copy-start(f32[8,256]{1,0:T(8,128)S(1)} %get-tuple-element.624) | copy-start | bytes 24580 | tf_op jit(solution)/shard_map/transpose(jvp())/while
  106.1 4.7 %copy-start.22 = (f32[8,256]{1,0:T(8,128)}, f32[8,256]{1,0:T(8,128)S(1)}, u32[]{:S(2)}) copy-start(f32[8,256]{1,0:T(8,128)S(1)} %get-tuple-element.626) | copy-start | bytes 24580 | tf_op jit(solution)/shard_map/transpose(jvp())/while
  117.6 4.7 %copy-start.21 = (f32[8,256]{1,0:T(8,128)}, f32[8,256]{1,0:T(8,128)S(1)}, u32[]{:S(2)}) copy-start(f32[8,256]{1,0:T(8,128)S(1)} %get-tuple-element.624) | copy-start | bytes 24580 | tf_op jit(solution)/shard_map/transpose(jvp())/while
  117.6 4.7 %copy-start.22 = (f32[8,256]{1,0:T(8,128)}, f32[8,256]{1,0:T(8,128)S(1)}, u32[]{:S(2)}) copy-start(f32[8,256]{1,0:T(8,128)S(1)} %get-tuple-element.626) | copy-start | bytes 24580 | tf_op jit(solution)/shard_map/transpose(jvp())/while
  129.1 4.7 %copy-start.21 = (f32[8,256]{1,0:T(8,128)}, f32[8,256]{1,0:T(8,128)S(1)}, u32[]{:S(2)}) copy-start(f32[8,256]{1,0:T(8,128)S(1)} %get-tuple-element.624) | copy-start | bytes 24580 | tf_op jit(solution)/shard_map/transpose(jvp())/while
  129.1 4.7 %copy-start.22 = (f32[8,256]{1,0:T(8,128)}, f32[8,256]{1,0:T(8,128)S(1)}, u32[]{:S(2)}) copy-start(f32[8,256]{1,0:T(8,128)S(1)} %get-tuple-element.626) | copy-start | bytes 24580 | tf_op jit(solution)/shard_map/transpose(jvp())/while
  140.6 4.7 %copy-start.21 = (f32[8,256]{1,0:T(8,128)}, f32[8,256]{1,0:T(8,128)S(1)}, u32[]{:S(2)}) copy-start(f32[8,256]{1,0:T(8,128)S(1)} %get-tuple-element.624) | copy-start | bytes 24580 | tf_op jit(solution)/shard_map/transpose(jvp())/while
  140.6 4.7 %copy-start.22 = (f32[8,256]{1,0:T(8,128)}, f32[8,256]{1,0:T(8,128)S(1)}, u32[]{:S(2)}) copy-start(f32[8,256]{1,0:T(8,128)S(1)} %get-tuple-element.626) | copy-start | bytes 24580 | tf_op jit(solution)/shard_map/transpose(jvp())/while
  153.8 3.4 %copy-start.24 = (f32[4,8,256]{2,1,0:T(8,128)S(1)}, f32[4,8,256]{2,1,0:T(8,128)}, u32[]{:S(2)}) copy-start(f32[4,8,256]{2,1,0:T(8,128)} %get-tuple-element.305) | copy-start | bytes 98308
  157.2 1.1 copy-start.9
  157.2 2.9 %copy-start.23 = (f32[256,32]{0,1:T(8,128)S(1)}, f32[256,32]{0,1:T(8,128)}, u32[]{:S(2)}) copy-start(f32[256,32]{0,1:T(8,128)} %get-tuple-element.472) | copy-start | bytes 98308
  157.2 3.6 %copy-start.7 = (f32[256,32]{1,0:T(8,128)S(1)}, f32[256,32]{1,0:T(8,128)}, u32[]{:S(2)}) copy-start(f32[256,32]{1,0:T(8,128)} %copy-done.6) | copy-start | bytes 98308
  157.2 3.6 %copy-start.14 = (f32[256,32]{1,0:T(8,128)S(1)}, f32[256,32]{1,0:T(8,128)}, u32[]{:S(2)}) copy-start(f32[256,32]{1,0:T(8,128)} %copy-done.13) | copy-start | bytes 98308
  158.0 17.0 %copy-start.11 = (bf16[256,288]{0,1:T(8,128)(2,1)S(1)}, bf16[256,288]{0,1:T(8,128)(2,1)}, u32[]{:S(2)}) copy-start(bf16[256,288]{0,1:T(8,128)(2,1)} %copy-done.10) | copy-start | bytes 442372
  158.0 17.2 %copy-start.18 = (f32[256,32]{0,1:T(8,128)S(1)}, f32[256,32]{0,1:T(8,128)}, u32[]{:S(2)}) copy-start(f32[256,32]{0,1:T(8,128)} %copy-done.17) | copy-start | bytes 98308
  175.0 4.6 %copy-start.19 = (f32[256,32]{1,0:T(8,128)}, f32[256,32]{1,0:T(8,128)S(1)}, u32[]{:S(2)}) copy-start(f32[256,32]{1,0:T(8,128)S(1)} %get-tuple-element.465) | copy-start | bytes 98308
  175.0 2.7 %copy-start.2 = (f32[256,2048]{0,1:T(8,128)S(1)}, f32[256,2048]{0,1:T(8,128)}, u32[]{:S(2)}) copy-start(f32[256,2048]{0,1:T(8,128)} %copy-done.1) | copy-start | bytes 6291460
  175.0 2.7 %copy-start.16 = (f32[256,32]{0,1:T(8,128)S(1)}, f32[256,32]{0,1:T(8,128)}, u32[]{:S(2)}) copy-start(f32[256,32]{0,1:T(8,128)} %copy-done.15) | copy-start | bytes 98308
  177.7 3.1 %copy-start.4 = (bf16[256,2048]{1,0:T(8,128)(2,1)S(1)}, bf16[256,2048]{1,0:T(8,128)(2,1)}, u32[]{:S(2)}) copy-start(bf16[256,2048]{1,0:T(8,128)(2,1)} %param.13) | copy-start | bytes 3145732
  177.7 3.1 %copy-start.5 = (bf16[256,2048]{1,0:T(8,128)(2,1)S(1)}, bf16[256,2048]{1,0:T(8,128)(2,1)}, u32[]{:S(2)}) copy-start(bf16[256,2048]{1,0:T(8,128)(2,1)} %param.19) | copy-start | bytes 3145732
  179.6 1.8 copy-start.33
  179.6 1.9 copy-start.12
  180.8 0.9 copy-start.20

commit v2 on v1

v2 whole, which is shorter than its diff:
```python
from functools import partial

import jax
import jax.numpy as jnp
from jax import lax
from jax.experimental import pallas as pl
from jax.experimental.pallas import tpu as pltpu
from jax.sharding import PartitionSpec as P


MESH = pl.DeviceIdType.MESH
CORES = 2
CHIPS = 4


def placing(length):
    here = lax.axis_index("seq")
    core = lax.rem(here, CORES)
    chip = lax.rem(lax.div(here, CORES), CHIPS)
    plane = lax.div(here, CORES * CHIPS)
    return core, chip, plane, length // (CORES * CHIPS)


def device_at(plane, chip, core):
    return {"seq": (plane * CHIPS + chip) * CORES + core}


def greet(length):
    core, chip, plane, planes = placing(length)
    barrier = pltpu.get_barrier_semaphore()
    others = [device_at(plane, chip, 1 - core)]
    others += [device_at(plane, lax.rem(chip + d, CHIPS), core) for d in range(1, CHIPS)]
    others += [device_at(lax.rem(plane + d, planes), chip, core) for d in range(1, planes)]
    for other in others:
        pl.semaphore_signal(barrier, inc=1, device_id=other, device_id_type=MESH)
    return lambda: pl.semaphore_wait(barrier, len(others))


def sending(src, dst, send, recv, at, to):
    return pltpu.make_async_remote_copy(
        src_ref=src,
        dst_ref=dst,
        send_sem=send.at[at],
        recv_sem=recv.at[at],
        device_id=to,
        device_id_type=MESH,
    )


def scan_states(length, width, own, out, pair, half, quad, part, zf, zb, gate, back, held, away,
                send, recv, keep, meanwhile):
    core, chip, plane, planes = placing(length)
    w = width
    heads = own.shape[0]
    mid, low = heads // CORES, heads // (CORES * CHIPS)
    partner = device_at(plane, chip, 1 - core)

    cp = sending(own.at[pl.ds((1 - core) * mid, mid)], pair.at[core], send, recv, 0, partner)
    cp.start()
    mine = pltpu.make_async_copy(own.at[pl.ds(core * mid, mid)], pair.at[core], keep.at[0])
    mine.start()
    mine.wait()
    cp.wait()
    first, second = 0, 1

    def join(h, _):
        f0, r0 = pair[first, h, 0:w], pair[first, h, w : w + 8]
        f1, r1 = pair[second, h, 0:w], pair[second, h, w : w + 8]
        a0, a1 = pair[first, h, w + 8 :], pair[second, h, w + 8 :]
        half[h, 0:w] = f1 + r1[0:1] * f0
        half[h, w : w + 8] = r0 * r1
        half[h, w + 8 :] = a0 + r0[0:1] * a1
        return 0

    lax.fori_loop(0, mid, join, 0)

    copies = []
    for d in range(1, CHIPS):
        to = lax.rem(chip + d, CHIPS)
        cp = sending(
            half.at[pl.ds(to * low, low)], quad.at[chip], send, recv, d, device_at(plane, to, core)
        )
        cp.start()
        copies.append(cp)
    mine = pltpu.make_async_copy(half.at[pl.ds(chip * low, low)], quad.at[chip], keep.at[1])
    mine.start()
    mine.wait()
    meanwhile(0)
    for cp in copies:
        cp.wait()

    def total(h, _):
        f, r = quad[0, h, 0:w], quad[0, h, w : w + 8]
        a = quad[CHIPS - 1, h, w + 8 :]
        for c in range(1, CHIPS):
            rc = quad[c, h, w : w + 8]
            f = quad[c, h, 0:w] + rc[0:1] * f
            r = r * rc
            e = CHIPS - 1 - c
            a = quad[e, h, w + 8 :] + quad[e, h, w : w + 1] * a
        part[h, 0:w] = f
        part[h, w : w + 8] = r
        part[h, w + 8 :] = a
        gate[h] = jnp.zeros((2 * w, gate.shape[2]), jnp.float32)
        return 0

    lax.fori_loop(0, low, total, 0)

    base = CHIPS
    ups, downs = [], []
    for d in range(1, planes):
        up = sending(
            part.at[:, 0 : w + 8], zf.at[d - 1], send, recv, base + d,
            device_at(lax.rem(plane + d, planes), chip, core),
        )
        down = sending(
            part.at[:, w : 2 * w + 8], zb.at[d - 1], send, recv, base + planes + d,
            device_at(lax.rem(plane + planes - d, planes), chip, core),
        )
        pl.when(plane + d < planes)(up.start)
        pl.when(plane - d >= 0)(down.start)
        ups.append(up)
        downs.append(down)
    meanwhile(1)
    for d in range(planes - 1, 0, -1):

        @pl.when(plane - d >= 0)
        def _():
            ups[d - 1].wait_recv()

            def add(h, _):
                gate[h, 0:w] = zf[d - 1, h, 0:w] + zf[d - 1, h, w : w + 1] * gate[h, 0:w]
                return 0

            lax.fori_loop(0, low, add, 0)

        @pl.when(plane + d < planes)
        def _():
            downs[d - 1].wait_recv()

            def add(h, _):
                gate[h, w:] = zb[d - 1, h, 8:] + zb[d - 1, h, 0:1] * gate[h, w:]
                return 0

            lax.fori_loop(0, low, add, 0)

    def spread(h, _):
        f, a = gate[h, 0:w], gate[h, w:]
        for c in range(CHIPS):
            e = CHIPS - 1 - c
            back[c, h, 0:w] = f
            back[e, h, w:] = a
            if c < CHIPS - 1:
                f = quad[c, h, 0:w] + quad[c, h, w : w + 1] * f
                a = quad[e, h, w + 8 :] + quad[e, h, w : w + 1] * a
        return 0

    lax.fori_loop(0, low, spread, 0)
    base = CHIPS + 2 * planes
    copies = []
    for d in range(1, CHIPS):
        to = lax.rem(chip + d, CHIPS)
        cp = sending(
            back.at[to], held.at[pl.ds(chip * low, low)], send, recv, base + d,
            device_at(plane, to, core),
        )
        cp.start()
        copies.append(cp)
    mine = pltpu.make_async_copy(back.at[chip], held.at[pl.ds(chip * low, low)], keep.at[2])
    mine.start()
    mine.wait()
    meanwhile(2)
    for cp in copies:
        cp.wait()

    def last(h, _):
        f, a = held[h, 0:w], held[h, w:]
        f1 = pair[first, h, 0:w] + pair[first, h, w : w + 1] * f
        a0 = pair[second, h, w + 8 :] + pair[second, h, w : w + 1] * a
        early = core == 0
        away[h, 0:w] = jnp.where(early, f1, f)
        away[h, w:] = jnp.where(early, a, a0)
        out[core * mid + h, 0:w] = jnp.where(early, f, f1)
        out[core * mid + h, w:] = jnp.where(early, a0, a)
        return 0

    lax.fori_loop(0, mid, last, 0)
    cp = sending(away, out.at[pl.ds(core * mid, mid)], send, recv, base + CHIPS, partner)
    cp.start()
    for d in range(1, planes):
        pl.when(plane + d < planes)(ups[d - 1].wait_send)
        pl.when(plane - d >= 0)(downs[d - 1].wait_send)
    cp.wait()


def sum_all(length, own, out, pair, half, quad, part, deep, send, recv):
    core, chip, plane, planes = placing(length)
    rows = own.shape[0]
    n1, n2, n3 = rows // CORES, rows // (CORES * CHIPS), rows // length
    partner = device_at(plane, chip, 1 - core)

    def across(copies):
        for cp in copies:
            cp.start()
        for cp in copies:
            cp.wait()

    across([sending(own.at[pl.ds((1 - core) * n1, n1)], pair, send, recv, 0, partner)])

    def first(i, _):
        at = pl.multiple_of(i * 64, 64)
        half[pl.ds(at, 64)] = own[pl.ds(core * n1 + at, 64)] + pair[pl.ds(at, 64)]
        return 0

    lax.fori_loop(0, n1 // 64, first, 0)
    chips = [lax.rem(chip + d, CHIPS) for d in range(1, CHIPS)]
    across(
        [
            sending(half.at[pl.ds(to * n2, n2)], quad.at[d], send, recv, 1 + d, device_at(plane, to, core))
            for d, to in enumerate(chips)
        ]
    )

    def second(i, _):
        at = pl.multiple_of(i * 64, 64)
        total = half[pl.ds(chip * n2 + at, 64)]
        for d in range(CHIPS - 1):
            total = total + quad[d, pl.ds(at, 64)]
        part[pl.ds(at, 64)] = total
        return 0

    lax.fori_loop(0, n2 // 64, second, 0)
    others = [lax.rem(plane + d, planes) for d in range(1, planes)]
    across(
        [
            sending(part.at[pl.ds(to * n3, n3)], deep.at[d], send, recv, CHIPS + d, device_at(to, chip, core))
            for d, to in enumerate(others)
        ]
    )
    total = part[pl.ds(plane * n3, n3)]
    for d in range(planes - 1):
        total = total + deep[d]
    at = core * n1 + chip * n2
    out[pl.ds(at + plane * n3, n3)] = total
    base = CHIPS + planes
    block = out.at[pl.ds(at + plane * n3, n3)]
    across(
        [
            sending(block, block, send, recv, base + d, device_at(to, chip, core))
            for d, to in enumerate(others)
        ]
    )
    block = out.at[pl.ds(at, n2)]
    base += planes
    across(
        [
            sending(block, block, send, recv, base + d, device_at(plane, to, core))
            for d, to in enumerate(chips)
        ]
    )
    block = out.at[pl.ds(core * n1, n1)]
    base += CHIPS
    across([sending(block, block, send, recv, base, partner)])


F32, BF16 = jnp.float32, jnp.bfloat16
LANES = 128
FAR = -1e30


def dot(a, b, dims=((1,), (0,)), precision=None):
    return lax.dot_general(
        a, b, (dims, ((), ())), preferred_element_type=F32, precision=precision
    )


def thirds(x, heads):
    high = x.astype(BF16)
    rest = x - high.astype(F32)
    mid = rest.astype(BF16)
    low = (rest - mid.astype(F32)).astype(BF16)
    keep = [part.astype(F32)[:, :heads] for part in (high, mid, low)]
    keep.append(jnp.zeros((x.shape[0], LANES - 3 * heads), F32))
    return jnp.concatenate(keep, axis=1).astype(BF16)


def layer_kernel(
    length, heads, tokens, values, weight, bias, decay_log, skip_gain, lengths, grad,
    output, grad_values, grad_tokens, total,
    own, states, pair, half, quad, part, zf, zb, gate, back, held, away, send, recv, keep,
    stack, s_pair, s_half, s_quad, s_part, s_deep, s_send, s_recv,
    scores, hidden, grad_scores, mixed, mixed_back, decays3, steps3, rows3, tails3, decays_t,
    b_map, c_map, sums, grad_maps, grad_gate,
):
    ready = greet(length)
    rows, inner = values.shape
    width = inner // heads
    state = (weight.shape[1] - heads) // 2
    pairs = inner // LANES
    per = LANES // width
    here = lax.axis_index("seq")
    first_row = here * rows

    down = lax.broadcasted_iota(jnp.int32, (rows, rows), 0)
    along = lax.broadcasted_iota(jnp.int32, (rows, rows), 1)
    at = first_row + lax.broadcasted_iota(jnp.int32, (rows, 1), 0)
    at_row = first_row + lax.broadcasted_iota(jnp.int32, (1, rows), 1)
    zero = jnp.zeros((rows, 1), jnp.int32)
    trace, trace_row, prior, final = (zero.astype(F32), jnp.zeros((1, rows), F32), zero.astype(F32), zero.astype(F32))
    end = 0
    for k in range(lengths.shape[0]):
        end = end + lengths[k]
        trace += jnp.where(at >= end, 1.0, 0.0)
        trace_row += jnp.where(at_row >= end, 1.0, 0.0)
        prior += jnp.where(zero + (first_row - 1) >= end, 1.0, 0.0)
        final += jnp.where(zero + (first_row + rows - 1) >= end, 1.0, 0.0)
    carrying = jnp.where(trace == prior, 1.0, 0.0)
    tail = jnp.where(trace == final, 1.0, 0.0)
    hidden[...] = jnp.where(down >= along, jnp.where(trace == trace_row, 0.0, FAR), FAR)
    lower = jnp.where(down >= along, 1.0, 0.0).astype(F32)

    projected = dot(tokens[...], weight[...])
    b = projected[:, :state].astype(BF16)
    c = projected[:, state : 2 * state].astype(BF16)
    b_map[...] = b
    c_map[...] = c
    fill = jnp.zeros((1, LANES - heads), F32)
    widen = lambda x: jnp.concatenate([x, jnp.broadcast_to(fill, (x.shape[0], LANES - heads))], axis=1)
    rate = widen(-jnp.exp(decay_log[...]))
    drive = widen(projected[:, 2 * state :] + bias[...])
    steps = jnp.maximum(drive, 0.0) + jnp.log1p(jnp.exp(-jnp.abs(drive)))
    decays = dot(lower, rate * steps, precision=lax.Precision.HIGHEST)
    last = decays[rows - 1 : rows]
    end_gap = jnp.exp(last - decays) * tail
    tails = end_gap * steps
    retained = jnp.exp(last) * carrying[rows - 1 : rows]
    scores[...] = dot(c, b, ((1,), (1,)))
    decays3[...] = thirds(decays, heads)
    steps3[...] = thirds(steps, heads)
    rows3[...] = thirds(jnp.exp(decays) * carrying, heads)
    tails3[...] = thirds(tails, heads)
    decays_t[...] = decays.T
    retained3 = thirds(jnp.broadcast_to(retained, (8, LANES)), heads)
    skip3 = thirds(jnp.broadcast_to(widen(skip_gain[...]), (8, LANES)), heads)
    b_t = b.astype(F32).T.astype(BF16)
    c_t = c.astype(F32).T.astype(BF16)

    up = lax.broadcasted_iota(jnp.int32, (LANES, LANES), 0)
    lane = lax.broadcasted_iota(jnp.int32, (LANES, LANES), 1)

    def spreading(i):
        return jnp.where((up % heads == per * i + lane // width) & (up < 3 * heads), 1.0, 0.0).astype(BF16)

    def columns(i):
        return pl.ds(pl.multiple_of(i * LANES, LANES), LANES)

    def prepare(i, _):
        hot = spreading(i)
        v = values[:, columns(i)].astype(F32)
        g = grad[:, columns(i)].astype(F32)
        w = (v * dot(tails3[...], hot)).astype(BF16)
        u = (g * dot(rows3[...], hot)).astype(BF16)
        own[i, 0:state] = dot(b_t, w)
        own[i, state : state + 8] = dot(retained3, hot)
        own[i, state + 8 :] = dot(c_t, u)
        return 0

    lax.fori_loop(0, pairs, prepare, 0)
    grad_scores[...] = jnp.zeros((rows, rows), F32)
    head_up = lax.broadcasted_iota(jnp.int32, (LANES, rows), 0)
    left = lax.broadcasted_iota(jnp.int32, (1, LANES), 1) // width

    def inside(i, _):
        v = values[:, columns(i)].astype(F32)
        g = grad[:, columns(i)]
        g_t = g.astype(F32).T.astype(BF16)
        scaled = v * dot(steps3[...], spreading(i))
        y = jnp.zeros((rows, LANES), F32)
        zs = []
        for e in range(per):
            h = per * i + e
            hot = jnp.where((head_up % heads == h) & (head_up < 3 * heads), 1.0, 0.0).astype(BF16)
            fade = jnp.exp(dot(decays3[...], hot) - decays_t[pl.ds(h, 1), :] + hidden[...])
            mixing = (scores[...] * fade).astype(BF16)
            one = jnp.where(left == e, scaled, 0.0).astype(BF16)
            grad_scores[...] += dot(g, one, ((1,), (1,))) * fade
            y = y + dot(mixing, one)
            zs.append(dot(g_t[e * width : (e + 1) * width], mixing))
        mixed[:, columns(i)] = y
        mixed_back[:, columns(i)] = jnp.concatenate(zs, axis=0).T
        return 0

    cuts = [0, pairs * 3 // 8, pairs * 6 // 8, pairs]

    def meanwhile(k):
        lax.fori_loop(cuts[k], cuts[k + 1], inside, 0)

    ready()
    scan_states(
        length, state, own, states, pair, half, quad, part, zf, zb, gate, back, held, away,
        send, recv, keep, meanwhile,
    )

    sums[...] = jnp.zeros(sums.shape, F32)
    grad_maps[...] = jnp.zeros(grad_maps.shape, F32)
    grad_gate[...] = jnp.zeros(grad_gate.shape, F32)
    tall = lax.broadcasted_iota(jnp.int32, (2 * LANES, LANES), 0)
    wide = lax.broadcasted_iota(jnp.int32, (2 * LANES, LANES), 1)

    def finish(i, _):
        hot = spreading(i)
        gather = jnp.where(wide == per * i + (tall % LANES) // width, 1.0, 0.0).astype(BF16)

        def by_head(x):
            high = x.astype(BF16)
            low = (x - high.astype(F32)).astype(BF16)
            return dot(jnp.concatenate([high, low], axis=1), gather)

        entering, adjoint = states[i, 0:state], states[i, state:]
        grad_gate[...] += by_head(
            jnp.broadcast_to(jnp.sum(entering * adjoint, axis=0, keepdims=True), (8, LANES))
        )
        entering, adjoint = entering.astype(BF16), adjoint.astype(BF16)
        v = values[:, columns(i)].astype(F32)
        g = grad[:, columns(i)].astype(F32)
        step, row, end = (dot(ref[...], hot) for ref in (steps3, rows3, tails3))
        skip = dot(skip3, hot)[0:1]
        carried = dot(c_map[...], entering) * row
        grad_weighted = dot(b_map[...], adjoint)
        y, z = mixed[:, columns(i)], mixed_back[:, columns(i)]
        weighted = v * end
        output[:, columns(i)] = (y + carried + skip * v).astype(BF16)
        grad_values[:, columns(i)] = (step * z + skip * g + grad_weighted * end).astype(BF16)
        grad_maps[0] += dot(weighted.astype(BF16), adjoint, ((1,), (1,)))
        grad_maps[1] += dot((g * row).astype(BF16), entering, ((1,), (1,)))
        scaled = (v * step).astype(BF16).astype(F32)
        sums[0] += by_head(g * (y + carried) - scaled * z - weighted * grad_weighted)
        sums[1] += by_head(v * z)
        sums[2] += by_head(v * grad_weighted)
        sums[3] += by_head(g * v)
        return 0

    lax.fori_loop(0, pairs, finish, 0)
    through = sums[2]
    grad_last = jnp.sum(tails * through, axis=0, keepdims=True) + retained * grad_gate[0:1]
    grad_rates = dot(lower, sums[0], ((0,), (0,)), lax.Precision.HIGHEST) + grad_last
    grad_steps = sums[1] + end_gap * through + rate * grad_rates
    grad_drive = grad_steps * jax.nn.sigmoid(drive)
    grad_s = grad_scores[...]
    grad_b = grad_maps[0] + dot(grad_s.T.astype(BF16), c)
    grad_c = grad_maps[1] + dot(grad_s.astype(BF16), b)
    grad_maps_b = jnp.concatenate([grad_b, grad_c], axis=1)
    rounded = grad_maps_b.astype(BF16)
    rounded_drive = grad_drive[:, :heads].astype(BF16)
    split = 2 * state
    flipped = jnp.concatenate([grad_maps_b.T, grad_drive.T[:heads]], axis=0).astype(BF16)
    blocks = tokens.shape[1] // LANES
    high, used = stack.shape[0] // blocks, split + heads
    for k in range(blocks):
        base = k * high
        stack[base : base + used] = dot(flipped, tokens[:, k * LANES : (k + 1) * LANES])
        stack[base + used : base + high] = jnp.zeros((high - used, LANES), F32)
    stack[used : used + 1] = jnp.sum(grad_drive, axis=0, keepdims=True)
    stack[used + 1 : used + 2] = rate * jnp.sum(
        grad_rates * steps, axis=0, keepdims=True
    )
    stack[used + 2 : used + 3] = jnp.sum(sums[3], axis=0, keepdims=True)

    grad_tokens[...] = (
        dot(rounded, weight[:, :split], ((1,), (1,)))
        + dot(rounded_drive, weight[:, split:], ((1,), (1,)))
    ).astype(BF16)
    sum_all(length, stack, total, s_pair, s_half, s_quad, s_part, s_deep, s_send, s_recv)


def shards(tokens, values, in_weight, step_bias, decay_log, skip_gain, trace_lengths, output_grad):
    row_count, inner = values.shape
    depth = tokens.shape[1]
    head_count = step_bias.shape[0]
    columns = in_weight.shape[1]
    state = (columns - head_count) // 2
    length = lax.axis_size("seq")
    planes = length // (CORES * CHIPS)
    pairs = inner // LANES
    mid, low = pairs // CORES, pairs // (CORES * CHIPS)
    tall = 2 * state + 8
    blocks = depth // LANES
    high = -(-(columns + 3) // 64) * 64
    lines = blocks * high
    n1, n2, n3 = lines // CORES, lines // (CORES * CHIPS), lines // length
    vmem = lambda *shape: pltpu.VMEM(shape, F32)
    half = lambda *shape: pltpu.VMEM(shape, BF16)
    here = pl.BlockSpec(memory_space=pltpu.VMEM)
    count = 2 * CHIPS + 2 * planes + 1
    output, grad_values, grad_tokens, total = pl.pallas_call(
        partial(layer_kernel, length, head_count),
        out_shape=(
            jax.ShapeDtypeStruct(values.shape, BF16),
            jax.ShapeDtypeStruct(values.shape, BF16),
            jax.ShapeDtypeStruct(tokens.shape, BF16),
            jax.ShapeDtypeStruct((lines, LANES), F32),
        ),
        in_specs=[here] * 6 + [pl.BlockSpec(memory_space=pltpu.SMEM), here],
        out_specs=(here,) * 4,
        scratch_shapes=[
            vmem(pairs, tall, LANES),
            vmem(pairs, 2 * state, LANES),
            vmem(CORES, mid, tall, LANES),
            vmem(mid, tall, LANES),
            vmem(CHIPS, low, tall, LANES),
            vmem(low, tall, LANES),
            vmem(planes - 1, low, state + 8, LANES),
            vmem(planes - 1, low, state + 8, LANES),
            vmem(low, 2 * state, LANES),
            vmem(CHIPS, low, 2 * state, LANES),
            vmem(mid, 2 * state, LANES),
            vmem(mid, 2 * state, LANES),
            pltpu.SemaphoreType.DMA((count,)),
            pltpu.SemaphoreType.DMA((count,)),
            pltpu.SemaphoreType.DMA((3,)),
            vmem(lines, LANES),
            vmem(n1, LANES),
            vmem(n1, LANES),
            vmem(CHIPS - 1, n2, LANES),
            vmem(n2, LANES),
            vmem(planes - 1, n3, LANES),
            pltpu.SemaphoreType.DMA((count,)),
            pltpu.SemaphoreType.DMA((count,)),
            vmem(row_count, row_count),
            vmem(row_count, row_count),
            vmem(row_count, row_count),
            vmem(row_count, inner),
            vmem(row_count, inner),
            half(row_count, LANES),
            half(row_count, LANES),
            half(row_count, LANES),
            half(row_count, LANES),
            vmem(LANES, row_count),
            half(row_count, state),
            half(row_count, state),
            vmem(4, row_count, LANES),
            vmem(2, row_count, state),
            vmem(8, LANES),
        ],
        compiler_params=pltpu.CompilerParams(
            collective_id=0, has_side_effects=True, vmem_limit_bytes=56 << 20
        ),
    )(
        tokens, values, in_weight, step_bias[None], decay_log[None], skip_gain[None],
        trace_lengths, output_grad,
    )
    total = total.reshape(blocks, high, LANES)
    grad_in_weight = total[:, :columns].transpose(0, 2, 1).reshape(depth, columns)
    grad_heads = total[0, columns : columns + 3, :head_count]
    return output, grad_values, grad_tokens, grad_in_weight, grad_heads


def solution(mesh):
    in_specs = (
        P(("groups", "seq"), None),
        P(("groups", "seq"), None),
        P(),
        P(),
        P(),
        P(),
        P("groups"),
        P(("groups", "seq"), None),
    )
    out_specs = (
        P(("groups", "seq"), None),
        P(("groups", "seq"), None),
        P(("groups", "seq"), None),
        P("groups", None),
        P("groups", None),
    )
    return jax.shard_map(shards, mesh=mesh, in_specs=in_specs, out_specs=out_specs, check_vma=False)
```

time: 218 us -> 111 us (0.51)
  local copies, waits for them, and re-layouts: 54.6 us -> 9.78 us
  matrix products: 43.8 us -> 0 us
  other arithmetic: 31.9 us -> 0 us
  Pallas kernels: 84.1 us -> 100 us
    dot_general x24 -> x0, matrix products: 43.8 us -> none  [the longest x12 27.8 us: head_block(): jnp.einsum('hij,jhp->ihp', mixing, head_vals, preferred_element_type=jnp....]
    pallas_call x2 -> x1, Pallas kernels: 84.1 us -> 100 us  [shards(): pl.pallas_call(partial(layer_kernel, length, head_count), out_shape=(jax....]
    dynamic_update_slice x12 -> x0, local copies, waits for them, and re-layouts: 11.4 us -> none  [respond(): lax.map(lambda pieces: kernel(pieces, linked, scores), (group_decay, grou...]
    add_any x6 -> x0, other arithmetic: 7.62 us -> none  [the longest x4 4.08 us: respond(): kernel(pieces, linked, scores)]
    another operation x11 -> x0, local copies, waits for them, and re-layouts: 7.1 us -> none
    another operation x7 -> x0, other arithmetic: 6.05 us -> none
    squeeze x8 -> x1, local copies, waits for them, and re-layouts: 7.15 us -> 1.34 us  [shards(): grad_heads = total[0, columns:columns + 3, :head_count]]
    reshape x6 -> x1, local copies, waits for them, and re-layouts: 8.04 us -> 2.43 us  [shards(): total[:, :columns].transpose(0, 2, 1).reshape(depth, columns)]
where the time goes in v2:
time: 111 us; the launch traced here: 110 us
  Pallas kernels  100 us (90%)
  local copies, waits for them, and re-layouts  9.78 us (9%)
    pallas_call x1, Pallas kernels, shards(): pl.pallas_call(partial(layer_kernel, length, head_count), out_shape=(jax....  100 us
    unnamed x10, local copies, waits for them, and re-layouts  6.02 us
    reshape x1, local copies, waits for them, and re-layouts, shards(): total[:, :columns].transpose(0, 2, 1).reshape(depth, columns)  2.43 us

profile of v2, /device:TPU:0, one launch (start us, length us, event | category | flops | bytes accessed | tf_op | source)
XLA Modules:
  0.0 110.5 jit_solution(2700254883991412394)
XLA Ops:
  0.6 2.2 %copy.13.weight = bf16[1024,288]{1,0:T(8,128)(2,1)} copy(bf16[1024,288]{0,1:T(8,128)(2,1)} %param.10) | data formatting | bytes 1179648 | tf_op args[2]
  2.9 100.0 %shard_map.119 = (bf16[256,2048]{1,0:T(8,128)(2,1)}, bf16[256,2048]{1,0:T(8,128)(2,1)}, bf16[256,1024]{1,0:T(8,128)(2,1)}, f32[2560,128]{1,0:T(8,128)}) custom-call(bf16[256,1024]{1,0:T(8,128)(2,1)} %tokens.1, bf16[256,2048]{1,0:T(8,128)(2,1)} %values.1, bf16[1024,288]{1,0:T(8,128)(2,1)} %copy.13.weight, f32[1,32]{1,0:T(1,128)} %bitcast.14, ...), custom_call_target="tpu_custom_call" | custom-call | tf_op jit(solution)/shard_map/pallas_call | solution.py:495
  102.9 0.0 copy-start.1
  102.9 1.3 %slice_bitcast_fusion.1 = f32[3,32]{1,0:T(4,128)} fusion(f32[8,320,128]{2,1,0:T(8,128)} %bitcast.12), kind=kLoop, calls=%fused_computation.2 | loop fusion | bytes 768 | tf_op jit(solution)/shard_map/squeeze | solution.py:554
  104.2 2.4 %copy_bitcast_fusion = f32[1024,288]{0,1:T(8,128)} fusion(f32[8,320,128]{2,1,0:T(8,128)} %bitcast.13), kind=kLoop, calls=%fused_computation | loop fusion | bytes 2359296 | tf_op jit(solution)/shard_map/reshape | solution.py:553
  106.7 0.0 copy-done.1
  106.7 0.0 copy-start
  106.7 1.0 copy.20
  107.6 0.6 copy-done
  108.3 0.0 copy-start.2
  108.3 1.0 copy.21
  109.2 0.4 copy-done.2
  109.7 0.8 copy.22
Async XLA Ops:
  102.9 3.8 %copy-start.1 = (bf16[256,2048]{1,0:T(8,128)(2,1)S(1)}, bf16[256,2048]{1,0:T(8,128)(2,1)}, u32[]{:S(2)}) copy-start(bf16[256,2048]{1,0:T(8,128)(2,1)} %get-tuple-element.18) | copy-start | bytes 3145732
  106.7 1.6 %copy-start = (bf16[256,2048]{1,0:T(8,128)(2,1)S(1)}, bf16[256,2048]{1,0:T(8,128)(2,1)}, u32[]{:S(2)}) copy-start(bf16[256,2048]{1,0:T(8,128)(2,1)} %get-tuple-element.19) | copy-start | bytes 3145732
  108.3 1.4 %copy-start.2 = (bf16[256,1024]{1,0:T(8,128)(2,1)S(1)}, bf16[256,1024]{1,0:T(8,128)(2,1)}, u32[]{:S(2)}) copy-start(bf16[256,1024]{1,0:T(8,128)(2,1)} %get-tuple-element.20) | copy-start | bytes 1572868

commit v3 on v2

--- a/solution.py
+++ b/solution.py
@@ -47,47 +47,53 @@
     )
 
 
-def scan_states(length, width, own, out, pair, half, quad, part, zf, zb, gate, back, held, away,
-                send, recv, keep, meanwhile):
-    core, chip, plane, planes = placing(length)
+def scan_stream(width, places, own, out, pair, half, quad, part, zf, zb, gate, back, held, away,
+                send, recv, keep):
+    core, chip, plane, planes = places
     w = width
     heads = own.shape[0]
     mid, low = heads // CORES, heads // (CORES * CHIPS)
     partner = device_at(plane, chip, 1 - core)
-
-    cp = sending(own.at[pl.ds((1 - core) * mid, mid)], pair.at[core], send, recv, 0, partner)
-    cp.start()
+    pending = []
+
+    def begin(cp):
+        cp.start()
+        pending.append(cp)
+
+    def settle():
+        for cp in pending:
+            cp.wait()
+        pending.clear()
+
+    begin(sending(own.at[pl.ds((1 - core) * mid, mid)], pair.at[core], send, recv, 0, partner))
+    yield
     mine = pltpu.make_async_copy(own.at[pl.ds(core * mid, mid)], pair.at[core], keep.at[0])
     mine.start()
     mine.wait()
-    cp.wait()
-    first, second = 0, 1
+    yield
+    settle()
 
     def join(h, _):
-        f0, r0 = pair[first, h, 0:w], pair[first, h, w : w + 8]
-        f1, r1 = pair[second, h, 0:w], pair[second, h, w : w + 8]
-        a0, a1 = pair[first, h, w + 8 :], pair[second, h, w + 8 :]
-        half[h, 0:w] = f1 + r1[0:1] * f0
+        r0, r1 = pair[0, h, w : w + 8], pair[1, h, w : w + 8]
+        half[h, 0:w] = pair[1, h, 0:w] + r1[0:1] * pair[0, h, 0:w]
         half[h, w : w + 8] = r0 * r1
-        half[h, w + 8 :] = a0 + r0[0:1] * a1
+        half[h, w + 8 :] = pair[0, h, w + 8 :] + r0[0:1] * pair[1, h, w + 8 :]
         return 0
 
     lax.fori_loop(0, mid, join, 0)
-
-    copies = []
-    for d in range(1, CHIPS):
-        to = lax.rem(chip + d, CHIPS)
-        cp = sending(
-            half.at[pl.ds(to * low, low)], quad.at[chip], send, recv, d, device_at(plane, to, core)
+    chips = [lax.rem(chip + d, CHIPS) for d in range(1, CHIPS)]
+    for d, to in enumerate(chips):
+        begin(
+            sending(
+                half.at[pl.ds(to * low, low)], quad.at[chip], send, recv, 1 + d,
+                device_at(plane, to, core),
+            )
         )
-        cp.start()
-        copies.append(cp)
     mine = pltpu.make_async_copy(half.at[pl.ds(chip * low, low)], quad.at[chip], keep.at[1])
     mine.start()
     mine.wait()
-    meanwhile(0)
-    for cp in copies:
-        cp.wait()
+    yield
+    settle()
 
     def total(h, _):
         f, r = quad[0, h, 0:w], quad[0, h, w : w + 8]
@@ -105,23 +111,21 @@
         return 0
 
     lax.fori_loop(0, low, total, 0)
-
-    base = CHIPS
     ups, downs = [], []
     for d in range(1, planes):
         up = sending(
-            part.at[:, 0 : w + 8], zf.at[d - 1], send, recv, base + d,
+            part.at[:, 0 : w + 8], zf.at[d - 1], send, recv, CHIPS + d,
             device_at(lax.rem(plane + d, planes), chip, core),
         )
         down = sending(
-            part.at[:, w : 2 * w + 8], zb.at[d - 1], send, recv, base + planes + d,
+            part.at[:, w : 2 * w + 8], zb.at[d - 1], send, recv, CHIPS + planes + d,
             device_at(lax.rem(plane + planes - d, planes), chip, core),
         )
         pl.when(plane + d < planes)(up.start)
         pl.when(plane - d >= 0)(down.start)
         ups.append(up)
         downs.append(down)
-    meanwhile(1)
+    yield
     for d in range(planes - 1, 0, -1):
 
         @pl.when(plane - d >= 0)
@@ -157,26 +161,23 @@
 
     lax.fori_loop(0, low, spread, 0)
     base = CHIPS + 2 * planes
-    copies = []
-    for d in range(1, CHIPS):
-        to = lax.rem(chip + d, CHIPS)
-        cp = sending(
-            back.at[to], held.at[pl.ds(chip * low, low)], send, recv, base + d,
-            device_at(plane, to, core),
+    for d, to in enumerate(chips):
+        begin(
+            sending(
+                back.at[to], held.at[pl.ds(chip * low, low)], send, recv, base + d,
+                device_at(plane, to, core),
+            )
         )
-        cp.start()
-        copies.append(cp)
     mine = pltpu.make_async_copy(back.at[chip], held.at[pl.ds(chip * low, low)], keep.at[2])
     mine.start()
     mine.wait()
-    meanwhile(2)
-    for cp in copies:
-        cp.wait()
+    yield
+    settle()
 
     def last(h, _):
         f, a = held[h, 0:w], held[h, w:]
-        f1 = pair[first, h, 0:w] + pair[first, h, w : w + 1] * f
-        a0 = pair[second, h, w + 8 :] + pair[second, h, w : w + 1] * a
+        f1 = pair[0, h, 0:w] + pair[0, h, w : w + 1] * f
+        a0 = pair[1, h, w + 8 :] + pair[1, h, w : w + 1] * a
         early = core == 0
         away[h, 0:w] = jnp.where(early, f1, f)
         away[h, w:] = jnp.where(early, a, a0)
@@ -185,87 +186,79 @@
         return 0
 
     lax.fori_loop(0, mid, last, 0)
-    cp = sending(away, out.at[pl.ds(core * mid, mid)], send, recv, base + CHIPS, partner)
-    cp.start()
+    begin(sending(away, out.at[pl.ds((core) * mid, mid)], send, recv, base + CHIPS, partner))
     for d in range(1, planes):
         pl.when(plane + d < planes)(ups[d - 1].wait_send)
         pl.when(plane - d >= 0)(downs[d - 1].wait_send)
-    cp.wait()
-
-
-def sum_all(length, own, out, pair, half, quad, part, deep, send, recv):
-    core, chip, plane, planes = placing(length)
+    yield
+    settle()
+    yield
+
+
+def sum_stream(length, places, own, out, pair, half, quad, part, deep, send, recv):
+    core, chip, plane, planes = places
     rows = own.shape[0]
     n1, n2, n3 = rows // CORES, rows // (CORES * CHIPS), rows // length
     partner = device_at(plane, chip, 1 - core)
-
-    def across(copies):
-        for cp in copies:
-            cp.start()
-        for cp in copies:
+    pending = []
+
+    def begin(src, dst, at, to):
+        cp = sending(src, dst, send, recv, at, to)
+        cp.start()
+        pending.append(cp)
+
+    def settle():
+        for cp in pending:
             cp.wait()
-
-    across([sending(own.at[pl.ds((1 - core) * n1, n1)], pair, send, recv, 0, partner)])
-
-    def first(i, _):
-        at = pl.multiple_of(i * 64, 64)
-        half[pl.ds(at, 64)] = own[pl.ds(core * n1 + at, 64)] + pair[pl.ds(at, 64)]
-        return 0
-
-    lax.fori_loop(0, n1 // 64, first, 0)
+        pending.clear()
+
+    begin(own.at[pl.ds((1 - core) * n1, n1)], pair, 0, partner)
+    yield
+    settle()
+    half[...] = own[pl.ds(core * n1, n1)] + pair[...]
     chips = [lax.rem(chip + d, CHIPS) for d in range(1, CHIPS)]
-    across(
-        [
-            sending(half.at[pl.ds(to * n2, n2)], quad.at[d], send, recv, 1 + d, device_at(plane, to, core))
-            for d, to in enumerate(chips)
-        ]
-    )
-
-    def second(i, _):
-        at = pl.multiple_of(i * 64, 64)
-        total = half[pl.ds(chip * n2 + at, 64)]
-        for d in range(CHIPS - 1):
-            total = total + quad[d, pl.ds(at, 64)]
-        part[pl.ds(at, 64)] = total
-        return 0
-
-    lax.fori_loop(0, n2 // 64, second, 0)
+    for d, to in enumerate(chips):
+        begin(half.at[pl.ds(to * n2, n2)], quad.at[d], 1 + d, device_at(plane, to, core))
+    yield
+    settle()
+    summed = half[pl.ds(chip * n2, n2)]
+    for d in range(CHIPS - 1):
+        summed = summed + quad[d]
+    part[...] = summed
     others = [lax.rem(plane + d, planes) for d in range(1, planes)]
-    across(
-        [
-            sending(part.at[pl.ds(to * n3, n3)], deep.at[d], send, recv, CHIPS + d, device_at(to, chip, core))
-            for d, to in enumerate(others)
-        ]
-    )
-    total = part[pl.ds(plane * n3, n3)]
+    for d, to in enumerate(others):
+        begin(part.at[pl.ds(to * n3, n3)], deep.at[d], CHIPS + d, device_at(to, chip, core))
+    yield
+    settle()
+    summed = part[pl.ds(plane * n3, n3)]
     for d in range(planes - 1):
-        total = total + deep[d]
+        summed = summed + deep[d]
     at = core * n1 + chip * n2
-    out[pl.ds(at + plane * n3, n3)] = total
+    out[pl.ds(at + plane * n3, n3)] = summed
     base = CHIPS + planes
     block = out.at[pl.ds(at + plane * n3, n3)]
-    across(
-        [
-            sending(block, block, send, recv, base + d, device_at(to, chip, core))
-            for d, to in enumerate(others)
-        ]
-    )
+    for d, to in enumerate(others):
+        begin(block, block, base + d, device_at(to, chip, core))
+    yield
+    settle()
     block = out.at[pl.ds(at, n2)]
     base += planes
-    across(
-        [
-            sending(block, block, send, recv, base + d, device_at(plane, to, core))
-            for d, to in enumerate(chips)
-        ]
-    )
+    for d, to in enumerate(chips):
+        begin(block, block, base + d, device_at(plane, to, core))
+    yield
+    settle()
     block = out.at[pl.ds(core * n1, n1)]
-    base += CHIPS
-    across([sending(block, block, send, recv, base, partner)])
+    begin(block, block, base + CHIPS, partner)
+    yield
+    settle()
+    yield
 
 
 F32, BF16 = jnp.float32, jnp.bfloat16
 LANES = 128
 FAR = -1e30
+STREAMS = 2
+SHARES = ((2, 3), (2, 3), (2, 4))
 
 
 def dot(a, b, dims=((1,), (0,)), precision=None):
@@ -286,16 +279,16 @@
 
 def layer_kernel(
     length, heads, tokens, values, weight, bias, decay_log, skip_gain, lengths, grad,
-    output, grad_values, grad_tokens, total,
+    output, grad_values, grad_tokens, grad_weight, grad_heads,
     own, states, pair, half, quad, part, zf, zb, gate, back, held, away, send, recv, keep,
-    stack, s_pair, s_half, s_quad, s_part, s_deep, s_send, s_recv,
+    stack, total, s_pair, s_half, s_quad, s_part, s_deep, s_send, s_recv,
     scores, hidden, grad_scores, mixed, mixed_back, decays3, steps3, rows3, tails3, decays_t,
     b_map, c_map, sums, grad_maps, grad_gate,
 ):
     ready = greet(length)
     rows, inner = values.shape
     width = inner // heads
-    state = (weight.shape[1] - heads) // 2
+    state = (weight.shape[0] - heads) // 2
     pairs = inner // LANES
     per = LANES // width
     here = lax.axis_index("seq")
@@ -319,7 +312,7 @@
     hidden[...] = jnp.where(down >= along, jnp.where(trace == trace_row, 0.0, FAR), FAR)
     lower = jnp.where(down >= along, 1.0, 0.0).astype(F32)
 
-    projected = dot(tokens[...], weight[...])
+    projected = dot(tokens[...], weight[...], ((1,), (1,)))
     b = projected[:, :state].astype(BF16)
     c = projected[:, state : 2 * state].astype(BF16)
     b_map[...] = b
@@ -365,7 +358,6 @@
         own[i, state + 8 :] = dot(c_t, u)
         return 0
 
-    lax.fori_loop(0, pairs, prepare, 0)
     grad_scores[...] = jnp.zeros((rows, rows), F32)
     head_up = lax.broadcasted_iota(jnp.int32, (LANES, rows), 0)
     left = lax.broadcasted_iota(jnp.int32, (1, LANES), 1) // width
@@ -390,16 +382,42 @@
         mixed_back[:, columns(i)] = jnp.concatenate(zs, axis=0).T
         return 0
 
-    cuts = [0, pairs * 3 // 8, pairs * 6 // 8, pairs]
-
-    def meanwhile(k):
-        lax.fori_loop(cuts[k], cuts[k + 1], inside, 0)
-
-    ready()
-    scan_states(
-        length, state, own, states, pair, half, quad, part, zf, zb, gate, back, held, away,
-        send, recv, keep, meanwhile,
-    )
+    places = placing(length)
+    core = places[0]
+    chunk = pairs // STREAMS
+    mid = chunk // CORES
+    done = 0
+
+    def meanwhile(amount):
+        nonlocal done
+        upto = min(pairs, done + amount)
+        lax.fori_loop(done, upto, inside, 0)
+        done = upto
+
+    streams = [
+        scan_stream(
+            state, places, own.at[pl.ds(q * chunk, chunk)], states.at[pl.ds(q * chunk, chunk)],
+            *(ref.at[q] for ref in (pair, half, quad, part, zf, zb, gate, back, held, away)),
+            send.at[q], recv.at[q], keep.at[q],
+        )
+        for q in range(STREAMS)
+    ]
+    for q in range(STREAMS):
+        theirs = q * chunk + (1 - core) * mid
+        lax.fori_loop(0, mid, lambda h, _: prepare(theirs + h, 0), 0)
+        if q == 0:
+            ready()
+        next(streams[q])
+        ours = q * chunk + core * mid
+        lax.fori_loop(0, mid, lambda h, _: prepare(ours + h, 0), 0)
+        next(streams[q])
+    for shares in SHARES:
+        for q in range(STREAMS):
+            next(streams[q])
+            meanwhile(shares[q] * pairs // 16)
+    meanwhile(pairs)
+    for q in range(STREAMS):
+        next(streams[q])
 
     sums[...] = jnp.zeros(sums.shape, F32)
     grad_maps[...] = jnp.zeros(grad_maps.shape, F32)
@@ -440,7 +458,12 @@
         sums[3] += by_head(g * v)
         return 0
 
-    lax.fori_loop(0, pairs, finish, 0)
+    for q in range(STREAMS):
+        ours = q * chunk + core * mid
+        lax.fori_loop(0, mid, lambda h, _: finish(ours + h, 0), 0)
+        next(streams[q])
+        theirs = q * chunk + (1 - core) * mid
+        lax.fori_loop(0, mid, lambda h, _: finish(theirs + h, 0), 0)
     through = sums[2]
     grad_last = jnp.sum(tails * through, axis=0, keepdims=True) + retained * grad_gate[0:1]
     grad_rates = dot(lower, sums[0], ((0,), (0,)), lax.Precision.HIGHEST) + grad_last
@@ -466,11 +489,27 @@
     )
     stack[used + 2 : used + 3] = jnp.sum(sums[3], axis=0, keepdims=True)
 
+    split_rows = stack.shape[0] // s_pair.shape[0]
+    streams = [
+        sum_stream(
+            length, places, stack.at[pl.ds(q * split_rows, split_rows)],
+            total.at[pl.ds(q * split_rows, split_rows)],
+            *(ref.at[q] for ref in (s_pair, s_half, s_quad, s_part, s_deep, s_send, s_recv)),
+        )
+        for q in range(s_pair.shape[0])
+    ]
+    for stream in streams:
+        next(stream)
     grad_tokens[...] = (
-        dot(rounded, weight[:, :split], ((1,), (1,)))
-        + dot(rounded_drive, weight[:, split:], ((1,), (1,)))
+        dot(rounded, weight[:split])
+        + dot(rounded_drive, weight[split:])
     ).astype(BF16)
-    sum_all(length, stack, total, s_pair, s_half, s_quad, s_part, s_deep, s_send, s_recv)
+    for _ in range(6):
+        for stream in streams:
+            next(stream)
+    for k in range(blocks):
+        grad_weight[:, k * LANES : (k + 1) * LANES] = total[k * high : k * high + used]
+    grad_heads[...] = total[used : used + 8]
 
 
 def shards(tokens, values, in_weight, step_bias, decay_log, skip_gain, trace_lengths, output_grad):
@@ -482,50 +521,54 @@
     length = lax.axis_size("seq")
     planes = length // (CORES * CHIPS)
     pairs = inner // LANES
-    mid, low = pairs // CORES, pairs // (CORES * CHIPS)
+    chunk = pairs // STREAMS
+    mid, low = chunk // CORES, chunk // (CORES * CHIPS)
     tall = 2 * state + 8
     blocks = depth // LANES
-    high = -(-(columns + 3) // 64) * 64
+    high = -(-(columns + 8) // 64) * 64
     lines = blocks * high
-    n1, n2, n3 = lines // CORES, lines // (CORES * CHIPS), lines // length
+    parts = 2 if lines % (16 * length) == 0 else 1
+    n1, n2, n3 = (lines // parts // k for k in (CORES, CORES * CHIPS, length))
     vmem = lambda *shape: pltpu.VMEM(shape, F32)
     half = lambda *shape: pltpu.VMEM(shape, BF16)
     here = pl.BlockSpec(memory_space=pltpu.VMEM)
     count = 2 * CHIPS + 2 * planes + 1
-    output, grad_values, grad_tokens, total = pl.pallas_call(
+    output, grad_values, grad_tokens, grad_weight, grad_heads = pl.pallas_call(
         partial(layer_kernel, length, head_count),
         out_shape=(
             jax.ShapeDtypeStruct(values.shape, BF16),
             jax.ShapeDtypeStruct(values.shape, BF16),
             jax.ShapeDtypeStruct(tokens.shape, BF16),
-            jax.ShapeDtypeStruct((lines, LANES), F32),
+            jax.ShapeDtypeStruct((columns, depth), F32),
+            jax.ShapeDtypeStruct((8, LANES), F32),
         ),
         in_specs=[here] * 6 + [pl.BlockSpec(memory_space=pltpu.SMEM), here],
-        out_specs=(here,) * 4,
+        out_specs=(here,) * 5,
         scratch_shapes=[
             vmem(pairs, tall, LANES),
             vmem(pairs, 2 * state, LANES),
-            vmem(CORES, mid, tall, LANES),
-            vmem(mid, tall, LANES),
-            vmem(CHIPS, low, tall, LANES),
-            vmem(low, tall, LANES),
-            vmem(planes - 1, low, state + 8, LANES),
-            vmem(planes - 1, low, state + 8, LANES),
-            vmem(low, 2 * state, LANES),
-            vmem(CHIPS, low, 2 * state, LANES),
-            vmem(mid, 2 * state, LANES),
-            vmem(mid, 2 * state, LANES),
-            pltpu.SemaphoreType.DMA((count,)),
-            pltpu.SemaphoreType.DMA((count,)),
-            pltpu.SemaphoreType.DMA((3,)),
+            vmem(STREAMS, CORES, mid, tall, LANES),
+            vmem(STREAMS, mid, tall, LANES),
+            vmem(STREAMS, CHIPS, low, tall, LANES),
+            vmem(STREAMS, low, tall, LANES),
+            vmem(STREAMS, planes - 1, low, state + 8, LANES),
+            vmem(STREAMS, planes - 1, low, state + 8, LANES),
+            vmem(STREAMS, low, 2 * state, LANES),
+            vmem(STREAMS, CHIPS, low, 2 * state, LANES),
+            vmem(STREAMS, mid, 2 * state, LANES),
+            vmem(STREAMS, mid, 2 * state, LANES),
+            pltpu.SemaphoreType.DMA((STREAMS, count)),
+            pltpu.SemaphoreType.DMA((STREAMS, count)),
+            pltpu.SemaphoreType.DMA((STREAMS, 3)),
             vmem(lines, LANES),
-            vmem(n1, LANES),
-            vmem(n1, LANES),
-            vmem(CHIPS - 1, n2, LANES),
-            vmem(n2, LANES),
-            vmem(planes - 1, n3, LANES),
-            pltpu.SemaphoreType.DMA((count,)),
-            pltpu.SemaphoreType.DMA((count,)),
+            vmem(lines, LANES),
+            vmem(parts, n1, LANES),
+            vmem(parts, n1, LANES),
+            vmem(parts, CHIPS - 1, n2, LANES),
+            vmem(parts, n2, LANES),
+            vmem(parts, planes - 1, n3, LANES),
+            pltpu.SemaphoreType.DMA((parts, count)),
+            pltpu.SemaphoreType.DMA((parts, count)),
             vmem(row_count, row_count),
             vmem(row_count, row_count),
             vmem(row_count, row_count),
@@ -546,13 +589,10 @@
             collective_id=0, has_side_effects=True, vmem_limit_bytes=56 << 20
         ),
     )(
-        tokens, values, in_weight, step_bias[None], decay_log[None], skip_gain[None],
+        tokens, values, in_weight.T, step_bias[None], decay_log[None], skip_gain[None],
         trace_lengths, output_grad,
     )
-    total = total.reshape(blocks, high, LANES)
-    grad_in_weight = total[:, :columns].transpose(0, 2, 1).reshape(depth, columns)
-    grad_heads = total[0, columns : columns + 3, :head_count]
-    return output, grad_values, grad_tokens, grad_in_weight, grad_heads
+    return output, grad_values, grad_tokens, grad_weight.T, grad_heads[:3, :head_count]
 
 
 def solution(mesh):

time: 111 us -> 86.9 us (0.78)
  Pallas kernels: 100 us -> 79.2 us
  local copies, waits for them, and re-layouts: 9.78 us -> 6.83 us
    pallas_call x1, Pallas kernels: 100 us -> 79.2 us  [shards(): pl.pallas_call(partial(layer_kernel, length, head_count), out_shape=(jax....]
    reshape x1 -> x0, local copies, waits for them, and re-layouts: 2.43 us -> none  [shards(): total[:, :columns].transpose(0, 2, 1).reshape(depth, columns)]
    slice x0 -> x1, local copies, waits for them, and re-layouts: none -> 1.35 us  [shards(): grad_heads[:3, :head_count]]
    squeeze x1 -> x0, local copies, waits for them, and re-layouts: 1.34 us -> none  [shards(): grad_heads = total[0, columns:columns + 3, :head_count]]
where the time goes in v3:
time: 86.9 us; the launch traced here: 86.6 us
  Pallas kernels  79.2 us (91%)
  local copies, waits for them, and re-layouts  6.83 us (8%)
    pallas_call x1, Pallas kernels, shards(): pl.pallas_call(partial(layer_kernel, length, head_count), out_shape=(jax....  79.2 us
    unnamed x10, local copies, waits for them, and re-layouts  5.49 us

profile of v3, /device:TPU:0, one launch (start us, length us, event | category | flops | bytes accessed | tf_op | source)
XLA Modules:
  0.0 86.6 jit_solution(8913137116243766410)
XLA Ops:
  0.6 79.2 %shard_map.119 = (bf16[256,2048]{1,0:T(8,128)(2,1)}, bf16[256,2048]{1,0:T(8,128)(2,1)}, bf16[256,1024]{1,0:T(8,128)(2,1)}, f32[288,1024]{1,0:T(8,128)}, f32[8,128]{1,0:T(8,128)}) custom-call(bf16[256,1024]{1,0:T(8,128)(2,1)} %tokens.1, bf16[256,2048]{1,0:T(8,128)(2,1)} %values.1, bf16[288,1024]{1,0:T(8,128)(2,1)} %bitcast.6, f32[1,32]{1,0:T(1,128)} %bitcast.7, ...), custom_call_target="tpu_custom_call" | custom-call | tf_op jit(solution)/shard_map/pallas_call | solution.py:536
  79.8 0.0 copy-start.1
  79.8 1.3 %slice.3 = f32[3,32]{1,0:T(4,128)} slice(f32[8,128]{1,0:T(8,128)} %get-tuple-element.14), slice={[0:3], [0:32]} | slice | bytes 768 | tf_op jit(solution)/shard_map/slice | solution.py:595
  81.2 2.3 %copy.17 = bf16[256,2048]{1,0:T(8,128)(2,1)} copy(bf16[256,2048]{1,0:T(8,128)(2,1)} %get-tuple-element.20) | data formatting | bytes 2097152
  83.5 0.0 copy-done.1
  83.5 0.0 copy-start.2
  83.5 0.0 copy-start
  83.5 1.0 %copy.18 = bf16[256,2048]{1,0:T(8,128)(2,1)} copy(bf16[256,2048]{1,0:T(8,128)(2,1)S(1)} %copy-done.1) | data formatting | bytes 2097152
  84.4 0.4 copy-done.2
  84.8 0.8 copy.19
  85.6 0.0 copy-done
  85.6 1.0 %copy.20 = f32[1024,288]{0,1:T(8,128)} copy(f32[1024,288]{0,1:T(8,128)S(1)} %bitcast.5) | data formatting | bytes 2359296
Async XLA Ops:
  79.8 3.7 %copy-start.1 = (bf16[256,2048]{1,0:T(8,128)(2,1)S(1)}, bf16[256,2048]{1,0:T(8,128)(2,1)}, u32[]{:S(2)}) copy-start(bf16[256,2048]{1,0:T(8,128)(2,1)} %get-tuple-element.21) | copy-start | bytes 3145732
  83.5 1.4 %copy-start.2 = (bf16[256,1024]{1,0:T(8,128)(2,1)S(1)}, bf16[256,1024]{1,0:T(8,128)(2,1)}, u32[]{:S(2)}) copy-start(bf16[256,1024]{1,0:T(8,128)(2,1)} %get-tuple-element.22) | copy-start | bytes 1572868
  83.5 2.2 %copy-start = (f32[288,1024]{1,0:T(8,128)S(1)}, f32[288,1024]{1,0:T(8,128)}, u32[]{:S(2)}) copy-start(f32[288,1024]{1,0:T(8,128)} %get-tuple-element.13) | copy-start | bytes 3538948

commit v4 on v3

--- a/solution.py
+++ b/solution.py
@@ -404,12 +404,12 @@
     ]
     for q in range(STREAMS):
         theirs = q * chunk + (1 - core) * mid
-        lax.fori_loop(0, mid, lambda h, _: prepare(theirs + h, 0), 0)
+        lax.fori_loop(0, mid, lambda h, _: prepare(theirs + h, 0), 0, unroll=2)
         if q == 0:
             ready()
         next(streams[q])
         ours = q * chunk + core * mid
-        lax.fori_loop(0, mid, lambda h, _: prepare(ours + h, 0), 0)
+        lax.fori_loop(0, mid, lambda h, _: prepare(ours + h, 0), 0, unroll=2)
         next(streams[q])
     for shares in SHARES:
         for q in range(STREAMS):
@@ -460,10 +460,10 @@
 
     for q in range(STREAMS):
         ours = q * chunk + core * mid
-        lax.fori_loop(0, mid, lambda h, _: finish(ours + h, 0), 0)
+        lax.fori_loop(0, mid, lambda h, _: finish(ours + h, 0), 0, unroll=2)
         next(streams[q])
         theirs = q * chunk + (1 - core) * mid
-        lax.fori_loop(0, mid, lambda h, _: finish(theirs + h, 0), 0)
+        lax.fori_loop(0, mid, lambda h, _: finish(theirs + h, 0), 0, unroll=2)
     through = sums[2]
     grad_last = jnp.sum(tails * through, axis=0, keepdims=True) + retained * grad_gate[0:1]
     grad_rates = dot(lower, sums[0], ((0,), (0,)), lax.Precision.HIGHEST) + grad_last
@@ -479,15 +479,18 @@
     flipped = jnp.concatenate([grad_maps_b.T, grad_drive.T[:heads]], axis=0).astype(BF16)
     blocks = tokens.shape[1] // LANES
     high, used = stack.shape[0] // blocks, split + heads
-    for k in range(blocks):
-        base = k * high
-        stack[base : base + used] = dot(flipped, tokens[:, k * LANES : (k + 1) * LANES])
-        stack[base + used : base + high] = jnp.zeros((high - used, LANES), F32)
+    stack[used : high] = jnp.zeros((high - used, LANES), F32)
     stack[used : used + 1] = jnp.sum(grad_drive, axis=0, keepdims=True)
     stack[used + 1 : used + 2] = rate * jnp.sum(
         grad_rates * steps, axis=0, keepdims=True
     )
     stack[used + 2 : used + 3] = jnp.sum(sums[3], axis=0, keepdims=True)
+
+    def fill(k):
+        base = k * high
+        stack[base : base + used] = dot(flipped, tokens[:, k * LANES : (k + 1) * LANES])
+        if k:
+            stack[base + used : base + high] = jnp.zeros((high - used, LANES), F32)
 
     split_rows = stack.shape[0] // s_pair.shape[0]
     streams = [
@@ -498,7 +501,11 @@
         )
         for q in range(s_pair.shape[0])
     ]
-    for stream in streams:
+    filled = 0
+    for q, stream in enumerate(streams):
+        while filled < blocks and filled * high < (q + 1) * split_rows:
+            fill(filled)
+            filled += 1
         next(stream)
     grad_tokens[...] = (
         dot(rounded, weight[:split])

time: 86.9 us -> 84.5 us (0.972)
  Pallas kernels: 79.2 us -> 76.8 us
    pallas_call x1, Pallas kernels: 79.2 us -> 76.8 us  [shards(): pl.pallas_call(partial(layer_kernel, length, head_count), out_shape=(jax....]
where the time goes in v4:
time: 84.5 us; the launch traced here: 84.3 us
  Pallas kernels  76.8 us (91%)
  local copies, waits for them, and re-layouts  6.83 us (8%)
    pallas_call x1, Pallas kernels, shards(): pl.pallas_call(partial(layer_kernel, length, head_count), out_shape=(jax....  76.8 us
    unnamed x10, local copies, waits for them, and re-layouts  5.49 us

profile of v4, /device:TPU:0, one launch (start us, length us, event | category | flops | bytes accessed | tf_op | source)
XLA Modules:
  0.0 84.3 jit_solution(3981575297383768209)
XLA Ops:
  0.6 76.8 %shard_map.119 = (bf16[256,2048]{1,0:T(8,128)(2,1)}, bf16[256,2048]{1,0:T(8,128)(2,1)}, bf16[256,1024]{1,0:T(8,128)(2,1)}, f32[288,1024]{1,0:T(8,128)}, f32[8,128]{1,0:T(8,128)}) custom-call(bf16[256,1024]{1,0:T(8,128)(2,1)} %tokens.1, bf16[256,2048]{1,0:T(8,128)(2,1)} %values.1, bf16[288,1024]{1,0:T(8,128)(2,1)} %bitcast.6, f32[1,32]{1,0:T(1,128)} %bitcast.7, ...), custom_call_target="tpu_custom_call" | custom-call | tf_op jit(solution)/shard_map/pallas_call | solution.py:543
  77.4 0.0 copy-start.1
  77.4 1.3 %slice.3 = f32[3,32]{1,0:T(4,128)} slice(f32[8,128]{1,0:T(8,128)} %get-tuple-element.14), slice={[0:3], [0:32]} | slice | bytes 768 | tf_op jit(solution)/shard_map/slice | solution.py:602
  78.8 2.3 %copy.17 = bf16[256,2048]{1,0:T(8,128)(2,1)} copy(bf16[256,2048]{1,0:T(8,128)(2,1)} %get-tuple-element.20) | data formatting | bytes 2097152
  81.1 0.0 copy-done.1
  81.1 0.0 copy-start.2
  81.1 0.0 copy-start
  81.1 1.0 %copy.18 = bf16[256,2048]{1,0:T(8,128)(2,1)} copy(bf16[256,2048]{1,0:T(8,128)(2,1)S(1)} %copy-done.1) | data formatting | bytes 2097152
  82.1 0.4 copy-done.2
  82.5 0.8 copy.19
  83.3 0.0 copy-done
  83.3 1.0 %copy.20 = f32[1024,288]{0,1:T(8,128)} copy(f32[1024,288]{0,1:T(8,128)S(1)} %bitcast.5) | data formatting | bytes 2359296
Async XLA Ops:
  77.4 3.7 %copy-start.1 = (bf16[256,2048]{1,0:T(8,128)(2,1)S(1)}, bf16[256,2048]{1,0:T(8,128)(2,1)}, u32[]{:S(2)}) copy-start(bf16[256,2048]{1,0:T(8,128)(2,1)} %get-tuple-element.21) | copy-start | bytes 3145732
  81.1 1.4 %copy-start.2 = (bf16[256,1024]{1,0:T(8,128)(2,1)S(1)}, bf16[256,1024]{1,0:T(8,128)(2,1)}, u32[]{:S(2)}) copy-start(bf16[256,1024]{1,0:T(8,128)(2,1)} %get-tuple-element.22) | copy-start | bytes 1572868
  81.1 2.2 %copy-start = (f32[288,1024]{1,0:T(8,128)S(1)}, f32[288,1024]{1,0:T(8,128)}, u32[]{:S(2)}) copy-start(f32[288,1024]{1,0:T(8,128)} %get-tuple-element.13) | copy-start | bytes 3538948

commit v5 on v4

--- a/solution.py
+++ b/solution.py
@@ -279,8 +279,8 @@
 
 def layer_kernel(
     length, heads, tokens, values, weight, bias, decay_log, skip_gain, lengths, grad,
-    output, grad_values, grad_tokens, grad_weight, grad_heads,
-    own, states, pair, half, quad, part, zf, zb, gate, back, held, away, send, recv, keep,
+    output_out, values_out, grad_tokens, grad_weight, grad_heads,
+    output, grad_values, leave, own, states, pair, half, quad, part, zf, zb, gate, back, held, away, send, recv, keep,
     stack, total, s_pair, s_half, s_quad, s_part, s_deep, s_send, s_recv,
     scores, hidden, grad_scores, mixed, mixed_back, decays3, steps3, rows3, tails3, decays_t,
     b_map, c_map, sums, grad_maps, grad_gate,
@@ -464,6 +464,12 @@
         next(streams[q])
         theirs = q * chunk + (1 - core) * mid
         lax.fori_loop(0, mid, lambda h, _: finish(theirs + h, 0), 0, unroll=2)
+    leaving = [
+        pltpu.make_async_copy(output, output_out, leave.at[0]),
+        pltpu.make_async_copy(grad_values, values_out, leave.at[1]),
+    ]
+    for cp in leaving:
+        cp.start()
     through = sums[2]
     grad_last = jnp.sum(tails * through, axis=0, keepdims=True) + retained * grad_gate[0:1]
     grad_rates = dot(lower, sums[0], ((0,), (0,)), lax.Precision.HIGHEST) + grad_last
@@ -517,6 +523,8 @@
     for k in range(blocks):
         grad_weight[:, k * LANES : (k + 1) * LANES] = total[k * high : k * high + used]
     grad_heads[...] = total[used : used + 8]
+    for cp in leaving:
+        cp.wait()
 
 
 def shards(tokens, values, in_weight, step_bias, decay_log, skip_gain, trace_lengths, output_grad):
@@ -534,7 +542,7 @@
     blocks = depth // LANES
     high = -(-(columns + 8) // 64) * 64
     lines = blocks * high
-    parts = 2 if lines % (16 * length) == 0 else 1
+    parts = 5 if lines % (40 * length) == 0 else 1
     n1, n2, n3 = (lines // parts // k for k in (CORES, CORES * CHIPS, length))
     vmem = lambda *shape: pltpu.VMEM(shape, F32)
     half = lambda *shape: pltpu.VMEM(shape, BF16)
@@ -550,8 +558,11 @@
             jax.ShapeDtypeStruct((8, LANES), F32),
         ),
         in_specs=[here] * 6 + [pl.BlockSpec(memory_space=pltpu.SMEM), here],
-        out_specs=(here,) * 5,
+        out_specs=(pl.BlockSpec(memory_space=pl.ANY),) * 2 + (here,) * 3,
         scratch_shapes=[
+            half(row_count, inner),
+            half(row_count, inner),
+            pltpu.SemaphoreType.DMA((2,)),
             vmem(pairs, tall, LANES),
             vmem(pairs, 2 * state, LANES),
             vmem(STREAMS, CORES, mid, tall, LANES),

time: 84.5 us -> 83.1 us (0.983)
  Pallas kernels: 76.8 us -> 75.4 us
    pallas_call x1, Pallas kernels: 76.8 us -> 75.4 us  [shards(): pl.pallas_call(partial(layer_kernel, length, head_count), out_shape=(jax....]
where the time goes in v5:
time: 83.1 us; the launch traced here: 82.9 us
  Pallas kernels  75.4 us (91%)
  local copies, waits for them, and re-layouts  6.83 us (8%)
    pallas_call x1, Pallas kernels, shards(): pl.pallas_call(partial(layer_kernel, length, head_count), out_shape=(jax....  75.4 us
    unnamed x10, local copies, waits for them, and re-layouts  5.49 us

profile of v5, /device:TPU:0, one launch (start us, length us, event | category | flops | bytes accessed | tf_op | source)
XLA Modules:
  0.0 82.9 jit_solution(12875516059199569660)
XLA Ops:
  0.6 75.4 %shard_map.119 = (bf16[256,2048]{1,0:T(8,128)(2,1)}, bf16[256,2048]{1,0:T(8,128)(2,1)}, bf16[256,1024]{1,0:T(8,128)(2,1)}, f32[288,1024]{1,0:T(8,128)}, f32[8,128]{1,0:T(8,128)}) custom-call(bf16[256,1024]{1,0:T(8,128)(2,1)} %tokens.1, bf16[256,2048]{1,0:T(8,128)(2,1)} %values.1, bf16[288,1024]{1,0:T(8,128)(2,1)} %bitcast.6, f32[1,32]{1,0:T(1,128)} %bitcast.7, ...), custom_call_target="tpu_custom_call" | custom-call | tf_op jit(solution)/shard_map/pallas_call | solution.py:551
  76.1 0.0 copy-start.1
  76.1 1.3 %slice.3 = f32[3,32]{1,0:T(4,128)} slice(f32[8,128]{1,0:T(8,128)} %get-tuple-element.14), slice={[0:3], [0:32]} | slice | bytes 768 | tf_op jit(solution)/shard_map/slice | solution.py:613
  77.4 2.3 %copy.17 = bf16[256,2048]{1,0:T(8,128)(2,1)} copy(bf16[256,2048]{1,0:T(8,128)(2,1)} %get-tuple-element.20) | data formatting | bytes 2097152
  79.7 0.0 copy-done.1
  79.7 0.0 copy-start.2
  79.7 0.0 copy-start
  79.7 1.0 %copy.18 = bf16[256,2048]{1,0:T(8,128)(2,1)} copy(bf16[256,2048]{1,0:T(8,128)(2,1)S(1)} %copy-done.1) | data formatting | bytes 2097152
  80.7 0.4 copy-done.2
  81.1 0.8 copy.19
  81.9 0.0 copy-done
  81.9 1.0 %copy.20 = f32[1024,288]{0,1:T(8,128)} copy(f32[1024,288]{0,1:T(8,128)S(1)} %bitcast.5) | data formatting | bytes 2359296
Async XLA Ops:
  76.1 3.7 %copy-start.1 = (bf16[256,2048]{1,0:T(8,128)(2,1)S(1)}, bf16[256,2048]{1,0:T(8,128)(2,1)}, u32[]{:S(2)}) copy-start(bf16[256,2048]{1,0:T(8,128)(2,1)} %get-tuple-element.21) | copy-start | bytes 3145732
  79.7 1.4 %copy-start.2 = (bf16[256,1024]{1,0:T(8,128)(2,1)S(1)}, bf16[256,1024]{1,0:T(8,128)(2,1)}, u32[]{:S(2)}) copy-start(bf16[256,1024]{1,0:T(8,128)(2,1)} %get-tuple-element.22) | copy-start | bytes 1572868
  79.7 2.2 %copy-start = (f32[288,1024]{1,0:T(8,128)S(1)}, f32[288,1024]{1,0:T(8,128)}, u32[]{:S(2)}) copy-start(f32[288,1024]{1,0:T(8,128)} %get-tuple-element.13) | copy-start | bytes 3538948
